TPU v7x, 256 devices: a whole 4x4x8 slice. The times are simulated.
256 devices in a mesh: real: 2 (over x_lo), bx: 16 (over y, x_hi, core), by: 8 (over z).
Axes of the slice: x: 4 (x_hi: 2, x_lo: 2; x = x_hi * 2 + x_lo), y: 4, z: 8, core: 2. Of those that a mesh axis runs over, the one named last changes fastest.
Arguments:
- current: float32 [2, 12, 3, 32, 64, 128], P('real', None, None, 'bx', 'by'), may hold values from -110 to 110
- previous: float32 [2, 12, 3, 32, 64, 128], P('real', None, None, 'bx', 'by'), may hold values from -110 to 110
- element_stiffness: float32 [24, 24], replicated, may hold values from -0.75 to 1.25, as said below
- preconditioner: float32 [2, 3, 32, 64, 128], P('real', None, 'bx', 'by'), may hold values from 0.04 to 0.16
- modulus: float32 [32, 64, 128], P('bx', 'by'), may hold values from 0.3 to 9.1
- density: float32 [32, 64, 128], P('bx', 'by'), may hold values from 0.5 to 2
- solid: int32 [2, 32, 64, 128], P('real', 'bx', 'by'), may hold values from 0 to 1, as said below
- clamped: int32 [32, 64], P('bx', 'by'), may hold values 0 or 1
Outputs:
- gram_stiff: float32 [2, 36, 36], P('real')
- gram_mass: float32 [2, 36, 36], P('real')
- search_block: float32 [2, 12, 3, 32, 64, 128], P('real', None, None, 'bx', 'by')
- sensitivity: float32 [32, 64, 128], P('bx', 'by', 'real')
Inputs may be any that keep to these rules, and one draw needn't show every extreme that they name: `element_stiffness`: symmetric positive definite: the stiffness of a trilinear brick of unit edge for unit modulus and a Poisson ratio between 0.25 and 0.35, divided by its diagonal entry, plus a small positive definite part. 1 marks a solid element of that realization; a realization's solid elements include those of every realization before it. `clamped`: 1 marks a bottom-face node held in all three directions.
All inputs are finite; a program needn't handle non-finite values. No bound on the sum of `clamped` on one device may be relied on, other than what follows from the above.
Results may differ from a plain program's by a relative error of at most 0.00013.
Values sent between devices are 32-bit elements; how exact they have to be, the bound alone decides.
A program may use at most 64 MiB of HBM per device.

v0:
```python
import functools

import jax
import jax.numpy as jnp
from jax import lax
from jax.sharding import Mesh
from jax.sharding import PartitionSpec as P

BX = ("bx_0", "bx_1", "bx_2")
BX_BY = ("bx_0", "bx_1", "bx_2", "by")


highest = lax.Precision.HIGHEST
soft_power = 4.0
group_width = 4
corner_list = [
    (0, 0, 0),
    (0, 0, 1),
    (0, 1, 0),
    (0, 1, 1),
    (1, 0, 0),
    (1, 0, 1),
    (1, 1, 0),
    (1, 1, 1),
]


def from_behind(value, axis, steps):
    count = lax.axis_size(axis)
    leading, last = (max(0, -steps), min(count, count - steps))
    return lax.ppermute(value, axis, [(source, source + steps) for source in range(leading, last)])


def over_axes(array, axes):
    return functools.reduce(lax.psum, axes, array)


def copy_for_each(array, axis):
    copies = jnp.broadcast_to(array, (lax.axis_size(axis), *array.shape))
    return lax.all_to_all(copies, axis, split_axis=0, concat_axis=0, tiled=True)


def of_everyone(array, axis):
    return copy_for_each(array, axis).sum(axis=0)


def split_up(array, dim, size):
    before, after = (array.shape[:dim], array.shape[dim + 1 :])
    return jnp.moveaxis(array.reshape(*before, size, -1, *after), dim, 0)


def sent_and_summed(array, axis, dim):
    pieces = split_up(array, dim, lax.axis_size(axis))
    arrived = lax.all_to_all(pieces, axis, split_axis=0, concat_axis=0, tiled=True)
    return arrived.sum(axis=0)


def corner_values(extended, size_x, size_y, size_z):
    return jnp.stack(
        [
            extended[
                ...,
                shift_x : shift_x + size_x,
                shift_y : shift_y + size_y,
                shift_z : shift_z + size_z,
            ]
            for shift_x, shift_y, shift_z in corner_list
        ],
        0,
    )


def scatter_corners(pieces):
    leading = pieces.ndim - 4
    overall = 0.0
    for corner, (shift_x, shift_y, shift_z) in enumerate(corner_list):
        widths = [(0, 0)] * leading + [
            (shift_x, 1 - shift_x),
            (shift_y, 1 - shift_y),
            (shift_z, 1 - shift_z),
        ]
        overall = overall + jnp.pad(pieces[corner], widths)
    return overall


def element_pass(extended, stiff_field, element_four):
    size_x, size_y, size_z = stiff_field.shape
    corner_vals = corner_values(extended, size_x, size_y, size_z)
    forces = jnp.einsum("adbe,bkexyz->akdxyz", element_four, corner_vals, precision=highest)
    energy_stiff = jnp.einsum("akdxyz,akdxyz->kxyz", corner_vals, forces, precision=highest)
    energy_mass = jnp.sum(corner_vals * corner_vals, axis=(0, 2)) * 0.125
    return (scatter_corners(forces * stiff_field), energy_stiff, energy_mass)


def grouped_pass(extended, stiff_field, element_four):
    columns = extended.shape[0]
    groups = extended.reshape((columns // group_width, group_width) + extended.shape[1:])

    def run_group(group_block):
        return element_pass(group_block, stiff_field, element_four)

    assembled, energy_stiff, energy_mass = lax.map(run_group, groups)
    return (
        assembled.reshape((columns,) + assembled.shape[2:]),
        energy_stiff.reshape((columns,) + energy_stiff.shape[2:]),
        energy_mass.reshape((columns,) + energy_mass.shape[2:]),
    )


def apply_block(block, stiff_field, free_mask, element_four):
    size_x, size_y, size_z = stiff_field.shape
    upper_rim = from_behind(block[:, :, :, 0:1], "by", -1)
    widened = jnp.concatenate([block, upper_rim], 3)
    beside = from_behind(widened[:, :, 0:1], BX, -1)
    widened = jnp.concatenate([widened, beside], 2)
    extended = jnp.pad(widened, ((0, 0), (0, 0), (0, 0), (0, 0), (0, 1)))
    assembled, energy_stiff, energy_mass = grouped_pass(extended, stiff_field, element_four)
    assembled = assembled[..., :size_z]
    spill_first = from_behind(assembled[:, :, size_x:], BX, 1)
    owned_part = jnp.concatenate([assembled[:, :, 0:1] + spill_first, assembled[:, :, 1:size_x]], 2)
    spill_second = from_behind(owned_part[:, :, :, size_y:], "by", 1)
    owned_part = jnp.concatenate(
        [owned_part[:, :, :, 0:1] + spill_second, owned_part[:, :, :, 1:size_y]], 3
    )
    return (owned_part * free_mask, energy_stiff, energy_mass)


def lumped_nodes(mass_rims, size_x, size_y, size_z):
    return scatter_corners(jnp.stack([mass_rims] * 8, 0))[1 : size_x + 1, 1 : size_y + 1, :size_z]


def gram_matrix(left_blocks, right_blocks):
    gram_rows = []
    for left_block in left_blocks:
        flat_left = left_block.reshape(left_block.shape[0], -1)
        gram_rows.append(
            jnp.concatenate(
                [
                    jnp.einsum(
                        "ik,jk->ij",
                        flat_left,
                        right_block.reshape(right_block.shape[0], -1),
                        precision=highest,
                    )
                    for right_block in right_blocks
                ],
                1,
            )
        )
    return jnp.concatenate(gram_rows, 0)


def combine_matrix(quotient, columns):
    eye_block = jnp.eye(columns, dtype=jnp.float32)
    zeros_block = jnp.zeros((columns, columns), jnp.float32)
    return jnp.concatenate(
        [
            jnp.concatenate([eye_block, zeros_block, zeros_block], 1),
            jnp.concatenate([zeros_block, eye_block, zeros_block], 1),
            jnp.concatenate([zeros_block, -jnp.diag(quotient), zeros_block], 1),
            jnp.concatenate([zeros_block, zeros_block, eye_block], 1),
        ],
        0,
    )


def shards(current, previous, element_stiffness, preconditioner, modulus, density, solid, clamped):
    element_four = element_stiffness.reshape(8, 3, 8, 3)
    size_x, size_y, size_z = modulus.shape
    columns = current.shape[1]
    dof_count = 3.0 * size_x * size_y * size_z * lax.axis_size(BX) * lax.axis_size("by")
    bottom = (jnp.arange(size_z) == 0).astype(jnp.float32)
    free_mask = 1.0 - clamped.astype(jnp.float32)[:, :, None] * bottom
    solid_share = solid[0].astype(jnp.float32)
    stiff_field = modulus * (0.02 + 0.98 * solid_share)
    mass_field = density * (0.1 + 0.9 * solid_share)
    mass_eighth = mass_field * 0.125
    below_x = from_behind(mass_eighth[size_x - 1 :], BX, 1)
    widened_mass = jnp.concatenate([below_x, mass_eighth], 0)
    below_y = from_behind(widened_mass[:, size_y - 1 :], "by", 1)
    mass_rims = jnp.concatenate([below_y, widened_mass], 1)
    lumped_free = lumped_nodes(mass_rims, size_x, size_y, size_z) * free_mask
    current_free = current[0] * free_mask
    previous_free = previous[0] * free_mask
    stiff_pair, energy_stiff, energy_mass = apply_block(
        jnp.concatenate([current_free, previous_free], 0), stiff_field, free_mask, element_four
    )
    stiff_cur = stiff_pair[:columns]
    stiff_prev = stiff_pair[columns:]
    mass_cur = lumped_free * current_free
    mass_prev = lumped_free * previous_free
    energy_stiff = energy_stiff[:columns]
    energy_mass = energy_mass[:columns]
    scaling = preconditioner[0][None]
    first_part = scaling * stiff_cur
    second_part = scaling * mass_cur
    stiff_both, _, _ = apply_block(
        jnp.concatenate([first_part, second_part], 0), stiff_field, free_mask, element_four
    )
    mass_first = lumped_free * first_part
    mass_second = lumped_free * second_part
    wide_basis = [current_free, first_part, second_part, previous_free]
    wide_stiff, wide_mass = (
        over_axes(
            gram_matrix(
                wide_basis, [stiff_cur, stiff_both[:columns], stiff_both[columns:], stiff_prev]
            )
            / dof_count,
            BX_BY,
        ),
        over_axes(
            gram_matrix(wide_basis, [mass_cur, mass_first, mass_second, mass_prev]) / dof_count,
            BX_BY,
        ),
    )
    denominator = jnp.diagonal(wide_mass)[:columns]
    quotient = jnp.diagonal(wide_stiff)[:columns] / denominator
    search = first_part - second_part * quotient[:, None, None, None, None]
    transform = combine_matrix(quotient, columns)
    gram_stiff = jnp.dot(
        transform.T, jnp.dot(wide_stiff, transform, precision=highest), precision=highest
    )
    gram_mass = jnp.dot(
        transform.T, jnp.dot(wide_mass, transform, precision=highest), precision=highest
    )
    powered = quotient ** (-soft_power)
    overall = of_everyone(jnp.sum(powered), "real")
    coefficient = powered / denominator
    local_terms = 3.0 * stiff_field * jnp.einsum(
        "j,jxyz->xyz", coefficient, energy_stiff, precision=highest
    ) - mass_field * jnp.einsum(
        "j,jxyz->xyz", coefficient * quotient, energy_mass, precision=highest
    )
    summed = sent_and_summed(local_terms, "real", 2)
    sensitivity = summed / overall
    return (gram_stiff[None], gram_mass[None], search[None], sensitivity)


def solution(mesh):
    split = Mesh(
        mesh.devices.reshape(mesh.shape["real"], 4, 2, 2, mesh.shape["by"]),
        ("real", "bx_0", "bx_1", "bx_2", "by"),
    )
    placed = (
        P("real", None, None, BX, "by", None),
        P("real", None, None, BX, "by", None),
        P(),
        P("real", None, BX, "by", None),
        P(BX, "by", None),
        P(BX, "by", None),
        P("real", BX, "by", None),
        P(BX, "by"),
    )
    return jax.shard_map(
        shards,
        mesh=split,
        in_specs=placed,
        out_specs=(
            P("real", None, None),
            P("real", None, None),
            P("real", None, None, BX, "by", None),
            P(BX, "by", "real"),
        ),
        check_vma=False,
    )
```

profile of v0, /device:TPU:2, one launch (start us, length us, event | category | flops | bytes accessed | tf_op | source)
XLA Modules:
  0.0 270.7 jit_solution(13346474767751798091)
XLA Ops:
  1.4 1.7 collective-permute-start.4
  3.9 3.8 %collective-permute-start.5 = (f32[3,1,128]{2,1,0:T(1,128)S(1)}, f32[3,1,128]{2,1,0:T(1,128)S(1)}, u32[]{:S(2)}, u32[]{:S(2)}) collective-permute-start(f32[3,1,128]{2,1,0:T(1,128)S(1)} %pad_maximum_fusion.10), channel_id=1, source_target_pairs={{0,1},{1,2},{2,3},{3,4},{4,5},{5,6},{6,7},{8,9},{9,10},{10,11},{11... | collective-permute-start | bytes 4616 | tf_op jit(solution)/shard_map/ppermute | solution.py:31
  14.9 3.5 %collective-permute-done = f32[24,3,2,1,128]{4,0,3,2,1:T(8,128)S(1)} collective-permute-done((f32[24,3,2,1,128]{4,0,3,2,1:T(8,128)S(1)}, f32[24,3,2,1,128]{4,0,3,2,1:T(8,128)S(1)}, u32[]{:S(2)}, u32[]{:S(2)}) %collective-permute-start) | collective-permute-done | bytes 73760 | tf_op jit(solution)/shard_map/ppermute | solution.py:31
  23.5 2.2 pad.145.clone
  25.8 2.2 broadcast.164.clone
  28.0 45.2 %while.28 = (s32[]{:T(128)}, f32[6,4,3,3,9,129]{5,4,3,2,1,0:T(8,128)}, f32[6,4,2,8,128]{4,3,2,1,0:T(8,128)}, f32[6,4,2,8,128]{4,3,2,1,0:T(8,128)}, f32[6,4,3,3,9...) while((s32[]{:T(128)}, ...), condition=%wide.region_2.3_spmd, body=%wide.region_0.2_spmd.sunk | while | flops 57890524 | bytes 14500745 | solution.py:102
  37.7 1.7 stack.110
  74.9 10.2 %collective-permute-start.2 = (f32[24,3,1,9,128]{4,0,3,2,1:T(8,128)S(1)}, f32[24,3,1,9,128]{4,0,3,2,1:T(8,128)S(1)}, u32[]{:S(2)}, u32[]{:S(2)}) collective-permute-start(f32[24,3,1,9,128]{4,0,3,2,1:T(8,128)S(1)} %copy.943), channel_id=1, source_target_pairs={{0,8},{8,16},{16,24},{24,32},{32,40},{40,48},{48,56},{56,64},{64,7... | collective-permute-start | bytes 995336 | tf_op jit(solution)/shard_map/ppermute | solution.py:31
  87.6 4.0 %collective-permute-start.3 = (f32[24,3,2,1,128]{4,0,3,2,1:T(8,128)S(1)}, f32[24,3,2,1,128]{4,0,3,2,1:T(8,128)S(1)}, u32[]{:S(2)}, u32[]{:S(2)}) collective-permute-start(f32[24,3,2,1,128]{4,0,3,2,1:T(8,128)S(1)} %pad_maximum_fusion.8), channel_id=1, source_target_pairs={{0,1},{1,2},{2,3},{3,4},{4,5},{5,6},{6,7},{8,9},{9,10},{10,11},{11... | collective-permute-start | bytes 221192 | tf_op jit(solution)/shard_map/ppermute | solution.py:31
  100.9 5.4 %collective-permute-done.6 = f32[24,3,2,1,128]{4,0,3,2,1:T(8,128)S(1)} collective-permute-done((f32[24,3,2,1,128]{4,0,3,2,1:T(8,128)S(1)}, f32[24,3,2,1,128]{4,0,3,2,1:T(8,128)S(1)}, u32[]{:S(2)}, u32[]{:S(2)}) %collective-permute-start.6) | collective-permute-done | bytes 73760 | tf_op jit(solution)/shard_map/ppermute | solution.py:31
  110.3 2.2 pad.154.clone
  112.6 2.2 broadcast.164
  114.8 39.3 %while.29 = (s32[]{:T(128)}, f32[6,4,3,3,9,129]{5,4,3,2,1,0:T(8,128)}, f32[6,4,3,3,9,129]{5,4,3,2,1,0:T(8,128)}, f32[8,3,8,3]{2,0,3,1:T(8,128)S(1)}, f32[2,8,128]{2,1,0:T(8,128)S(1)}, /*index=5*/s32[]{:T(128)}) while((s32[]{:T(128)}, f32[6,4,3,3,9,129]{5,4,3,2,1,0:T(8,128)}, f32[6,4,3,3,9,129]{5,4,3,2,1,0:T(8,128)}, ...), condition=%wide.region_4.5_spmd, body=%wide.region_3.4_spmd.sunk | while | flops 57112284 | bytes 11158389 | solution.py:102
  123.5 1.7 stack.111
  143.2 1.7 stack.111
  155.8 10.9 %collective-permute-start.8 = (f32[24,3,1,9,128]{4,0,3,2,1:T(8,128)S(1)}, f32[24,3,1,9,128]{4,0,3,2,1:T(8,128)S(1)}, u32[]{:S(2)}, u32[]{:S(2)}) collective-permute-start(f32[24,3,1,9,128]{4,0,3,2,1:T(8,128)S(1)} %copy.946), channel_id=1, source_target_pairs={{0,8},{8,16},{16,24},{24,32},{32,40},{40,48},{48,56},{56,64},{64,7... | collective-permute-start | bytes 995336 | tf_op jit(solution)/shard_map/ppermute | solution.py:31
  169.0 5.1 %collective-permute-start.9 = (f32[24,3,2,1,128]{4,0,3,2,1:T(8,128)S(1)}, f32[24,3,2,1,128]{4,0,3,2,1:T(8,128)S(1)}, u32[]{:S(2)}, u32[]{:S(2)}) collective-permute-start(f32[24,3,2,1,128]{4,0,3,2,1:T(8,128)S(1)} %pad_maximum_fusion.6), channel_id=1, source_target_pairs={{0,1},{1,2},{2,3},{3,4},{4,5},{5,6},{6,7},{8,9},{9,10},{10,11},{11... | collective-permute-start | bytes 221192 | tf_op jit(solution)/shard_map/ppermute | solution.py:31
  174.2 1.8 collective-permute-done.9
  181.5 23.8 %all-reduce.29 = (f32[48,48]{1,0:T(8,128)S(1)}, f32[48,48]{1,0:T(8,128)S(1)}) all-reduce(f32[48,48]{1,0:T(8,128)S(1)} %maximum_multiply_fusion, f32[48,48]{1,0:T(8,128)S(1)} %maximum_multiply_fusion.1), channel_id=1, replica_groups=mesh['real'=2,'bx_0'=4,'bx_1'=2,'bx_2'=2,'by'=8] {'bx_0'}, use_global_device_ids=true, to_apply=%region_5.6 | all-reduce | flops 4608 | bytes 36864 | tf_op jit(solution)/shard_map/psum | solution.py:35
  205.4 8.7 %all-reduce.31 = (f32[48,48]{1,0:T(8,128)S(1)}, f32[48,48]{1,0:T(8,128)S(1)}) all-reduce(f32[48,48]{1,0:T(8,128)S(1)} %get-tuple-element.398, f32[48,48]{1,0:T(8,128)S(1)} %get-tuple-element.399), channel_id=1, replica_groups=mesh['real'=2,'bx_0'=4,'bx_1'=2,'bx_2'=2,'by'=8] {'bx_1'}, use_global_device_ids=true, to_apply=%region_6.7 | all-reduce | flops 4608 | bytes 36864 | tf_op jit(solution)/shard_map/psum | solution.py:35
  214.0 3.5 %all-reduce.30 = (f32[48,48]{1,0:T(8,128)S(1)}, f32[48,48]{1,0:T(8,128)S(1)}) all-reduce(f32[48,48]{1,0:T(8,128)S(1)} %get-tuple-element.402, f32[48,48]{1,0:T(8,128)S(1)} %get-tuple-element.403), channel_id=1, replica_groups=mesh['real'=2,'bx_0'=4,'bx_1'=2,'bx_2'=2,'by'=8] {'bx_2'}, use_global_device_ids=true, to_apply=%region_7.8 | all-reduce | flops 4608 | bytes 36864 | tf_op jit(solution)/shard_map/psum | solution.py:35
  217.6 31.8 %all-reduce.28 = (f32[48,48]{1,0:T(8,128)S(1)}, f32[48,48]{1,0:T(8,128)S(1)}) all-reduce(f32[48,48]{1,0:T(8,128)S(1)} %get-tuple-element.400, f32[48,48]{1,0:T(8,128)S(1)} %get-tuple-element.401), channel_id=1, replica_groups=mesh['real'=2,'bx_0'=4,'bx_1'=2,'bx_2'=2,'by'=8] {'by'}, use_global_device_ids=true, to_apply=%region_8.9 | all-reduce | flops 4608 | bytes 36864 | tf_op jit(solution)/shard_map/psum | solution.py:35
  255.0 4.9 %all_to_all.11 = f32[2,1,1]{2,1,0:T(1,128)S(1)} all-to-all(f32[2,1,1]{2,1,0:T(1,128)S(1)} %broadcast_in_dim.76), channel_id=1, replica_groups=mesh['real'=2,'bx_0'=4,'bx_1'=2,'bx_2'=2,'by'=8] {'real'}, dimensions={0} | all-to-all | bytes 16 | tf_op jit(solution)/shard_map/all_to_all | solution.py:40
  260.0 5.2 %all-to-all-start = ((f32[2,1,1024]{2,1,0:T(1,128)}), f32[2,1,1024]{2,1,0:T(1,128)S(1)}, u32[]{:S(2)}, u32[]{:S(2)}) async-start(f32[2,1,1024]{2,1,0:T(1,128)} %reshape.186), calls=%async_computation | async-start | bytes 16384 | tf_op jit(solution)/shard_map/all_to_all | solution.py:54
  (369 shorter events, 129.3 us)
Async XLA Ops:
  1.4 2.6 collective-permute-start.4
  3.9 5.5 %collective-permute-start.5 = (f32[3,1,128]{2,1,0:T(1,128)S(1)}, f32[3,1,128]{2,1,0:T(1,128)S(1)}, u32[]{:S(2)}, u32[]{:S(2)}) collective-permute-start(f32[3,1,128]{2,1,0:T(1,128)S(1)} %pad_maximum_fusion.10), channel_id=1, source_target_pairs={{0,1},{1,2},{2,3},{3,4},{4,5},{5,6},{6,7},{8,9},{9,10},{10,11},{11... | collective-permute-start | bytes 4616 | tf_op jit(solution)/shard_map/ppermute | solution.py:31
  12.1 6.2 %collective-permute-start = (f32[24,3,2,1,128]{4,0,3,2,1:T(8,128)S(1)}, f32[24,3,2,1,128]{4,0,3,2,1:T(8,128)S(1)}, u32[]{:S(2)}, u32[]{:S(2)}) collective-permute-start(f32[24,3,2,1,128]{4,0,3,2,1:T(8,128)S(1)} %pad_maximum_fusion.9), channel_id=1, source_target_pairs={{1,0},{2,1},{3,2},{4,3},{5,4},{6,5},{7,6},{9,8},{10,9},{11,10},{12... | collective-permute-start | bytes 221192 | tf_op jit(solution)/shard_map/ppermute | solution.py:31
  18.4 4.7 %collective-permute-start.1 = (f32[24,3,1,9,128]{4,0,3,2,1:T(8,128)S(1)}, f32[24,3,1,9,128]{4,0,3,2,1:T(8,128)S(1)}, u32[]{:S(2)}, u32[]{:S(2)}) collective-permute-start(f32[24,3,1,9,128]{4,0,3,2,1:T(8,128)S(1)} %pad_maximum_fusion.4), channel_id=1, source_target_pairs={{8,0},{16,8},{24,16},{32,24},{40,32},{48,40},{56,48},{64,56},{72,6... | collective-permute-start | bytes 995336 | tf_op jit(solution)/shard_map/ppermute | solution.py:31
  74.8 17.5 %copy-start.5 = (f32[6,4,2,8,128]{4,3,2,1,0:T(8,128)S(1)}, f32[6,4,2,8,128]{4,3,2,1,0:T(8,128)}, u32[]{:S(2)}) copy-start(f32[6,4,2,8,128]{4,3,2,1,0:T(8,128)} %get-tuple-element.163) | copy-start | bytes 589828
  74.8 18.2 %copy-start.6 = (f32[6,4,2,8,128]{4,3,2,1,0:T(8,128)S(1)}, f32[6,4,2,8,128]{4,3,2,1,0:T(8,128)}, u32[]{:S(2)}) copy-start(f32[6,4,2,8,128]{4,3,2,1,0:T(8,128)} %get-tuple-element.162) | copy-start | bytes 589828
  74.9 12.5 %collective-permute-start.2 = (f32[24,3,1,9,128]{4,0,3,2,1:T(8,128)S(1)}, f32[24,3,1,9,128]{4,0,3,2,1:T(8,128)S(1)}, u32[]{:S(2)}, u32[]{:S(2)}) collective-permute-start(f32[24,3,1,9,128]{4,0,3,2,1:T(8,128)S(1)} %copy.943), channel_id=1, source_target_pairs={{0,8},{8,16},{16,24},{24,32},{32,40},{40,48},{48,56},{56,64},{64,7... | collective-permute-start | bytes 995336 | tf_op jit(solution)/shard_map/ppermute | solution.py:31
  86.6 7.1 %copy-start = (f32[1,12,3,2,8,128]{5,4,3,2,1,0:T(8,128)S(1)}, f32[1,12,3,2,8,128]{5,4,3,2,1,0:T(8,128)}, u32[]{:S(2)}) copy-start(f32[1,12,3,2,8,128]{5,4,3,2,1,0:T(8,128)} %param.12) | copy-start | bytes 884740
  86.6 7.1 %copy-start.2 = (f32[1,3,2,8,128]{4,3,2,1,0:T(8,128)S(1)}, f32[1,3,2,8,128]{4,3,2,1,0:T(8,128)}, u32[]{:S(2)}) copy-start(f32[1,3,2,8,128]{4,3,2,1,0:T(8,128)} %param.15) | copy-start | bytes 73732
  87.3 7.1 %copy-start.1 = (f32[1,12,3,2,8,128]{5,4,3,2,1,0:T(8,128)S(1)}, f32[1,12,3,2,8,128]{5,4,3,2,1,0:T(8,128)}, u32[]{:S(2)}) copy-start(f32[1,12,3,2,8,128]{5,4,3,2,1,0:T(8,128)} %param.13) | copy-start | bytes 884740
  87.6 6.0 %collective-permute-start.3 = (f32[24,3,2,1,128]{4,0,3,2,1:T(8,128)S(1)}, f32[24,3,2,1,128]{4,0,3,2,1:T(8,128)S(1)}, u32[]{:S(2)}, u32[]{:S(2)}) collective-permute-start(f32[24,3,2,1,128]{4,0,3,2,1:T(8,128)S(1)} %pad_maximum_fusion.8), channel_id=1, source_target_pairs={{0,1},{1,2},{2,3},{3,4},{4,5},{5,6},{6,7},{8,9},{9,10},{10,11},{11... | collective-permute-start | bytes 221192 | tf_op jit(solution)/shard_map/ppermute | solution.py:31
  99.0 7.4 %collective-permute-start.6 = (f32[24,3,2,1,128]{4,0,3,2,1:T(8,128)S(1)}, f32[24,3,2,1,128]{4,0,3,2,1:T(8,128)S(1)}, u32[]{:S(2)}, u32[]{:S(2)}) collective-permute-start(f32[24,3,2,1,128]{4,0,3,2,1:T(8,128)S(1)} %pad_maximum_fusion.7), channel_id=1, source_target_pairs={{1,0},{2,1},{3,2},{4,3},{5,4},{6,5},{7,6},{9,8},{10,9},{11,10},{12... | collective-permute-start | bytes 221192 | tf_op jit(solution)/shard_map/ppermute | solution.py:31
  106.4 3.6 %collective-permute-start.7 = (f32[24,3,1,9,128]{4,0,3,2,1:T(8,128)S(1)}, f32[24,3,1,9,128]{4,0,3,2,1:T(8,128)S(1)}, u32[]{:S(2)}, u32[]{:S(2)}) collective-permute-start(f32[24,3,1,9,128]{4,0,3,2,1:T(8,128)S(1)} %pad_maximum_fusion.2), channel_id=1, source_target_pairs={{8,0},{16,8},{24,16},{32,24},{40,32},{48,40},{56,48},{64,56},{72,6... | collective-permute-start | bytes 995336 | tf_op jit(solution)/shard_map/ppermute | solution.py:31
  155.7 18.4 %copy-start.7 = (f32[12,12]{1,0:T(8,128)S(1)}, f32[12,12]{1,0:T(8,128)}, u32[]{:S(2)}) copy-start(f32[12,12]{1,0:T(8,128)} %convolution_bitcast_fusion.6) | copy-start | bytes 1732
  155.7 18.4 %copy-start.8 = (f32[12,12]{1,0:T(8,128)S(1)}, f32[12,12]{1,0:T(8,128)}, u32[]{:S(2)}) copy-start(f32[12,12]{1,0:T(8,128)} %convolution_bitcast_fusion.16) | copy-start | bytes 1732
  155.8 13.0 %collective-permute-start.8 = (f32[24,3,1,9,128]{4,0,3,2,1:T(8,128)S(1)}, f32[24,3,1,9,128]{4,0,3,2,1:T(8,128)S(1)}, u32[]{:S(2)}, u32[]{:S(2)}) collective-permute-start(f32[24,3,1,9,128]{4,0,3,2,1:T(8,128)S(1)} %copy.946), channel_id=1, source_target_pairs={{0,8},{8,16},{16,24},{24,32},{32,40},{40,48},{48,56},{56,64},{64,7... | collective-permute-start | bytes 995336 | tf_op jit(solution)/shard_map/ppermute | solution.py:31
  169.0 7.1 %collective-permute-start.9 = (f32[24,3,2,1,128]{4,0,3,2,1:T(8,128)S(1)}, f32[24,3,2,1,128]{4,0,3,2,1:T(8,128)S(1)}, u32[]{:S(2)}, u32[]{:S(2)}) collective-permute-start(f32[24,3,2,1,128]{4,0,3,2,1:T(8,128)S(1)} %pad_maximum_fusion.6), channel_id=1, source_target_pairs={{0,1},{1,2},{2,3},{3,4},{4,5},{5,6},{6,7},{8,9},{9,10},{10,11},{11... | collective-permute-start | bytes 221192 | tf_op jit(solution)/shard_map/ppermute | solution.py:31
  178.0 74.2 %copy-start.12 = (f32[12,12]{1,0:T(8,128)S(1)}, f32[12,12]{1,0:T(8,128)}, u32[]{:S(2)}) copy-start(f32[12,12]{1,0:T(8,128)} %fusion.74) | copy-start | bytes 1732
  178.0 74.8 %copy-start.3 = (f32[3,4,2,8,128]{4,3,2,1,0:T(8,128)S(1)}, f32[3,4,2,8,128]{4,3,2,1,0:T(8,128)}, u32[]{:S(2)}) copy-start(f32[3,4,2,8,128]{4,3,2,1,0:T(8,128)} %slice.314) | copy-start | bytes 294916
  178.1 75.0 %copy-start.4 = (f32[3,4,2,8,128]{4,3,2,1,0:T(8,128)S(1)}, f32[3,4,2,8,128]{4,3,2,1,0:T(8,128)}, u32[]{:S(2)}) copy-start(f32[3,4,2,8,128]{4,3,2,1,0:T(8,128)} %slice.312) | copy-start | bytes 294916
  178.1 75.5 %copy-start.9 = (f32[2,8,128]{2,1,0:T(8,128)S(1)}, f32[2,8,128]{2,1,0:T(8,128)}, u32[]{:S(2)}) copy-start(f32[2,8,128]{2,1,0:T(8,128)} %param.17) | copy-start | bytes 24580
  178.1 75.5 %copy-start.10 = (s32[1,2,8,128]{3,2,1,0:T(8,128)S(1)}, s32[1,2,8,128]{3,2,1,0:T(8,128)}, u32[]{:S(2)}) copy-start(s32[1,2,8,128]{3,2,1,0:T(8,128)} %param.18) | copy-start | bytes 24580
  178.1 75.5 %copy-start.11 = (f32[2,8,128]{2,1,0:T(8,128)S(1)}, f32[2,8,128]{2,1,0:T(8,128)}, u32[]{:S(2)}) copy-start(f32[2,8,128]{2,1,0:T(8,128)} %param.16) | copy-start | bytes 24580
  260.0 8.2 %all-to-all-start = ((f32[2,1,1024]{2,1,0:T(1,128)}), f32[2,1,1024]{2,1,0:T(1,128)S(1)}, u32[]{:S(2)}, u32[]{:S(2)}) async-start(f32[2,1,1024]{2,1,0:T(1,128)} %reshape.186), calls=%async_computation | async-start | bytes 16384 | tf_op jit(solution)/shard_map/all_to_all | solution.py:54
where the time goes:
time: 273 us; the launch traced here: 271 us
  local copies, waits for them, and re-layouts  74.3 us (27%)
  blocking collectives  72.8 us (27%)
  starting transfers between devices  46.1 us (17%)
  matrix products  34 us (12%)
  other arithmetic  29.4 us (11%)
  waiting for transfers between devices  11.4 us (4%)
    psum x4, blocking collectives, over_axes(): return functools.reduce(lax.psum, axes, array)  67.9 us
    ppermute x10, starting transfers between devices, from_behind(): lax.ppermute(value, axis, [(source, source + steps) for source in range(l...  40.9 us
    another operation x120, local copies, waits for them, and re-layouts, corner_values(): jnp.stack([extended[..., shift_x:shift_x + size_x, shift_y:shift_y + size...  32.5 us
    dot_general x32, matrix products, gram_matrix(): jnp.einsum('ik,jk->ij', flat_left, right_block.reshape(right_block.shape[...  22.5 us
    dynamic_update_slice x18, other arithmetic, grouped_pass(): assembled, energy_stiff, energy_mass = lax.map(run_group, groups)  18.2 us
    squeeze x12, local copies, waits for them, and re-layouts, grouped_pass(): assembled, energy_stiff, energy_mass = lax.map(run_group, groups)  13.2 us
    ppermute x10, waiting for transfers between devices, from_behind(): lax.ppermute(value, axis, [(source, source + steps) for source in range(l...  11.4 us
    dot_general x12, matrix products, element_pass(): jnp.einsum('adbe,bkexyz->akdxyz', element_four, corner_vals, precision=hi...  9.85 us
  transfers between devices with their start and end apart: 11, of which 5 were waited for; matrix products, arithmetic and copies ran while one was open for 7% of the time, Pallas kernels for 0%

commit v1 on v0

v1 whole, which is shorter than its diff:
```python
import functools

import jax
import jax.numpy as jnp
import numpy as np
from jax import lax
from jax.experimental import pallas as pl
from jax.experimental.pallas import tpu as pltpu
from jax.sharding import PartitionSpec as P

MESH = pl.DeviceIdType.MESH
F32 = jnp.float32
BF16 = jnp.bfloat16
COLS = 12
WIDE = 4 * COLS
PAIRS = COLS // 2
DIRS = [
    (1, 0, (0, 2), (0, 8), 3, 0),
    (-1, 0, (1, 1), (0, 8), 0, 0),
    (0, 1, (0, 2), (0, 2), 1, 8),
    (0, -1, (0, 2), (7, 1), 1, 10),
    (1, 1, (0, 2), (0, 2), 3, 8),
    (1, -1, (0, 2), (7, 1), 3, 10),
    (-1, 1, (1, 1), (0, 2), 0, 8),
    (-1, -1, (1, 1), (7, 1), 0, 10),
]
PREV_DIRS = [
    (1, 0, (0, 1), (0, 8), 2, 0),
    (0, 1, (0, 2), (0, 1), 0, 8),
    (1, 1, (0, 1), (0, 1), 2, 8),
]


def operator_tables():
    pick_row = np.zeros((256, 24), np.float32)
    pick_col = np.zeros((24, 384), np.float32)
    allow = np.zeros((2, 256, 192), np.float32)
    row_y = np.full(256, 99)
    row_b = np.zeros(256, int)
    for a in range(2):
        for b in range(2):
            for q in range(2):
                for d in range(3):
                    i = 3 * (4 * a + 2 * b + q) + d
                    for y in range(8):
                        m = a * 128 + ((b * 2 + q) * 3 + d) * 8 + y
                        pick_row[m, i], row_y[m], row_b[m] = 1, y, b
                    m = a * 128 + 96 + (b * 2 + q) * 8 + d
                    pick_row[m, i], row_y[m], row_b[m] = 1, 8, b
    for a in range(2):
        for d in range(3):
            for q in range(2):
                for row in range(11):
                    k = a * 96 + (d * 2 + q) * 16 + row
                    y = -1 if row == 10 else row
                    for b in range(2):
                        pick_col[3 * (4 * a + 2 * b + q) + d, b * 192 + k] = 1
                        allow[b, :, k] = (y - row_y + row_b == b).astype(np.float32)
    return pick_row, pick_col, allow


def pair_dot(left, right):
    return lax.dot_general(left, right, (((1,), (0,)), ((), ())), preferred_element_type=F32)


def exact_dot(left, right):
    return lax.dot_general(
        left,
        right,
        (((1,), (0,)), ((), ())),
        preferred_element_type=F32,
        precision=lax.Precision.HIGHEST,
    )


def halves(value):
    high = value.astype(BF16)
    return high, (value - high.astype(F32)).astype(BF16)


def lane_of(value):
    return lax.broadcasted_iota(jnp.int32, value.shape, 1)


def row_of(value):
    return lax.broadcasted_iota(jnp.int32, value.shape, 0)


def from_next_z(value):
    return jnp.where(lane_of(value) == 127, 0.0, pltpu.roll(value, 127, 1))


def to_next_z(value):
    return jnp.where(lane_of(value) == 0, 0.0, pltpu.roll(value, 1, 1))


def spread(row):
    return jnp.broadcast_to(row, (8, 128))


def from_lower_y(main, below):
    return jnp.where(row_of(main) == 0, spread(below), pltpu.roll(main, 1, 0))


def from_upper_y(main, above):
    return jnp.where(row_of(main) == 7, spread(above), pltpu.roll(main, 7, 0))


def stacked_rows(rows):
    out = jnp.zeros((8, 128), F32)
    at = row_of(out)
    for d, row in enumerate(rows):
        out = jnp.where(at == d, spread(row), out)
    return out


def halo_copies(sizes, refs, sems):
    bx, by = lax.axis_index("bx"), lax.axis_index("by")
    nx, ny = sizes
    send_sem, recv_sem = sems
    out = []
    jobs = [(DIRS, refs["fld"], refs["FE"]), (DIRS, refs["cur"], refs["XC"])]
    jobs.append((PREV_DIRS, refs["prev"], refs["XP"]))
    for dirs, source, target in jobs:
        for dx, dy, (x0, xn), (y0, yn), tx, ty in dirs:
            to_x, to_y = bx - dx, by - dy
            sends = (to_x >= 0) & (to_x < nx) & (to_y >= 0) & (to_y < ny)
            gets = (bx + dx >= 0) & (bx + dx < nx) & (by + dy >= 0) & (by + dy < ny)
            at = len(out)
            copy = pltpu.make_async_remote_copy(
                src_ref=source.at[:, :, x0 : x0 + xn, y0 : y0 + yn, :],
                dst_ref=target.at[:, :, tx : tx + xn, ty : ty + yn, :],
                send_sem=send_sem.at[at],
                recv_sem=recv_sem.at[at],
                device_id={"bx": to_x, "by": to_y},
                device_id_type=MESH,
            )
            out.append((copy, sends, gets))
    return out


N_HALO = 2 * len(DIRS) + len(PREV_DIRS)


def greet_neighbours(sizes, barrier):
    bx, by = lax.axis_index("bx"), lax.axis_index("by")
    nx, ny = sizes
    count = 0
    for dx in (-1, 0, 1):
        for dy in (-1, 0, 1):
            if dx == 0 and dy == 0:
                continue
            there = (bx + dx >= 0) & (bx + dx < nx) & (by + dy >= 0) & (by + dy < ny)

            @pl.when(there)
            def _():
                pl.semaphore_signal(
                    barrier,
                    inc=1,
                    device_id={"bx": bx + dx, "by": by + dy},
                    device_id_type=MESH,
                )

            count = count + there.astype(jnp.int32)
    return count


def local_copies(refs, sem):
    return [
        pltpu.make_async_copy(refs["fld"], refs["FE"].at[:, :, 1:3, 0:8, :], sem.at[0]),
        pltpu.make_async_copy(refs["cur"], refs["XC"].at[:, :, 1:3, 0:8, :], sem.at[1]),
        pltpu.make_async_copy(refs["prev"], refs["XP"].at[:, :, 0:2, 0:8, :], sem.at[2]),
    ]


def build_operator(refs):
    spread_rows = exact_dot(refs["pick_row"][...], refs["elem"][...])
    both = exact_dot(spread_rows, refs["pick_col"][...])
    full = refs["allow"][0] * both[:, 0:192] + refs["allow"][1] * both[:, 192:384]
    high, low = halves(full)
    for a in range(2):
        refs["WH"][a] = high[a * 128 : a * 128 + 128]
        refs["WL"][a] = low[a * 128 : a * 128 + 128]


def halo_kernel(sizes, names, *args):
    refs = dict(zip(names, args))
    for name in ("XC", "XP", "FE"):
        ref = refs[name]
        for i in range(ref.shape[0]):
            ref[i] = jnp.zeros(ref.shape[1:], F32)
    barrier = pltpu.get_barrier_semaphore()
    count = greet_neighbours(sizes, barrier)
    locals_ = local_copies(refs, refs["local_sem"])
    for copy in locals_:
        copy.start()
    pl.semaphore_wait(barrier, count)
    copies = halo_copies(sizes, refs, (refs["send_sem"], refs["recv_sem"]))
    for copy, sends, _ in copies:
        pl.when(sends)(copy.start)
    build_operator(refs)
    for copy in locals_:
        copy.wait()
    for copy, sends, gets in copies:
        pl.when(gets)(copy.wait_recv)
    for copy, sends, gets in copies:
        pl.when(sends)(copy.wait_send)


def prepare_fields(refs):
    FE, SS, LM, PM, P8 = refs["FE"], refs["SS"], refs["LM"], refs["PM"], refs["P8"]
    mass_sum = []
    for e in range(4):
        for kind in range(2):
            main, row8 = FE[0, kind, e, 0:8], FE[0, kind, e, 8:9]
            below = FE[0, kind, e, 10:11]
            lower = from_lower_y(main, below)
            here8, lower8 = spread(row8), spread(main[7:8])
            if kind == 0:
                SS[e, 0], SS[e, 1], SS[e, 2], SS[e, 3] = main, lower, here8, lower8
            else:
                mass_sum.append((main + lower, here8 + lower8))
    for n in range(3):
        for part in range(2):
            total = mass_sum[n][part] + mass_sum[n + 1][part]
            keep = FE[0, 2, n + 1, 0:8] if part == 0 else spread(FE[0, 2, n + 1, 8:9])
            LM[n, part] = (total + to_next_z(total)) * 0.125 * keep
        for d in range(3):
            PM[n, d] = FE[1, d, n + 1, 0:8] * FE[0, 2, n + 1, 0:8]
        P8[n] = stacked_rows([FE[1, d, n + 1, 8:9] * FE[0, 2, n + 1, 8:9] for d in range(3)])


def store_operand(high_ref, low_ref, lead, d, h, value):
    for q, plane in enumerate((value, from_next_z(value))):
        high, low = halves(plane)
        at = (*lead, slice((d * 2 + q) * 16, (d * 2 + q) * 16 + 16), slice(h * 128, h * 128 + 128))
        high_ref[at] = high
        low_ref[at] = low


def forces(refs, a, high, low):
    return (
        pair_dot(refs["WH"][a], high)
        + pair_dot(refs["WH"][a], low)
        + pair_dot(refs["WL"][a], high)
    )


def block_of(force, b, q, d, h):
    g = ((b * 2 + q) * 3 + d) * 8
    return force[g : g + 8, h * 128 : h * 128 + 128]


def block8_of(force, b, q, h):
    g = 96 + (b * 2 + q) * 8
    return force[g : g + 8, h * 128 : h * 128 + 128]


def add_to(store, key, value):
    store[key] = value if key not in store else store[key] + value


def current_pair(refs, p):
    XC, FE, VV, UH, UL = refs["XC"], refs["FE"], refs["VV"], refs["UH"], refs["UL"]
    SS, LM, PM, P8 = refs["SS"], refs["LM"], refs["PM"], refs["P8"]
    XS, KS, X8, K8 = refs["XS"], refs["KS"], refs["X8"], refs["K8"]
    for h in range(2):
        for x in range(5):
            keep = FE[0, 2, x]
            for d in range(3):
                value = XC[2 * p + h, d, x] * keep
                store_operand(UH, UL, (x,), d, h, value)
                VV[h, d, 0, x] = value
                VV[h, d, 1, x] = from_next_z(value)
    edge = {}
    for h in range(2):
        for q in range(2):
            for x in range(1, 4):
                edge[h, q, x] = stacked_rows([VV[h, d, q, x, 8:9] for d in range(3)])
    total, total8, energy, energy8 = {}, {}, {}, {}
    for e in range(4):
        high = UH[e : e + 2].reshape(192, 256)
        low = UL[e : e + 2].reshape(192, 256)
        for a in range(2):
            n = e - 1 + a
            if not 0 <= n <= 2:
                continue
            force = forces(refs, a, high, low)
            for h in range(2):
                for b in range(2):
                    for q in range(2):
                        for d in range(3):
                            block = block_of(force, b, q, d, h)
                            add_to(total, (n, d, q, h), SS[e, b] * block)
                            if e in (1, 2):
                                add_to(energy, (e, b, h), VV[h, d, q, e + a, 0:8] * block)
                        block = block8_of(force, b, q, h)
                        add_to(total8, (n, q, h), SS[e, 2 + b] * block)
                        if e in (1, 2) and b == 1:
                            add_to(energy8, (e, h), edge[h, q, e + a] * block)
    zero = jnp.zeros((8, 128), F32)
    for h in range(2):
        c = 2 * p + h
        for n in range(3):
            stiff8 = total8[n, 0, h] + to_next_z(total8[n, 1, h])
            first8 = P8[n] * stiff8
            second8 = P8[n] * LM[n, 1] * edge[h, 0, n + 1]
            for ref, col, value in (
                (X8, 0, edge[h, 0, n + 1]),
                (X8, 1, first8),
                (X8, 2, second8),
                (K8, 0, zero),
            ):
                ref[n, pl.ds(pl.multiple_of((col * COLS + c) * 8, 8), 8), :] = value
            for d in range(3):
                stiff = total[n, d, 0, h] + to_next_z(total[n, d, 1, h])
                here = VV[h, d, 0, n + 1, 0:8]
                first = PM[n, d] * stiff
                second = PM[n, d] * LM[n, 0] * here
                for ref, col, value in (
                    (XS, 0, here),
                    (XS, 1, first),
                    (XS, 2, second),
                    (KS, 0, stiff if n < 2 else zero),
                ):
                    at = pl.ds(pl.multiple_of((col * COLS + c) * 8, 8), 8)
                    ref[d * 3 + n, at, :] = value
                if n < 2:
                    refs["first"][c, d, n] = first
                    refs["second"][c, d, n] = second
                for kind, main, row8 in ((0, first, first8), (1, second, second8)):
                    plane = jnp.concatenate([main, spread(row8[d : d + 1])], 0)
                    store_operand(refs["U2H"], refs["U2L"], (kind * PAIRS + p, n), d, h, plane)
        for e in (1, 2):
            above = jnp.sum(energy8[e, h], axis=0, keepdims=True)
            refs["ES"][c, e - 1] = energy[e, 0, h] + from_upper_y(energy[e, 1, h], above)
            square = 0.0
            for x in (e, e + 1):
                for d in range(3):
                    for q in range(2):
                        square = square + VV[h, d, q, x] * VV[h, d, q, x]
            main = square[0:8]
            refs["EM"][c, e - 1] = (main + from_upper_y(main, square[8:9])) * 0.125


def previous_pair(refs, p):
    for h in range(2):
        c = 2 * p + h
        at = pl.ds(pl.multiple_of((3 * COLS + c) * 8, 8), 8)
        for n in range(3):
            rows = []
            for d in range(3):
                value = refs["XP"][c, d, n] * refs["FE"][0, 2, n + 1]
                store_operand(refs["U2H"], refs["U2L"], (2 * PAIRS + p, n), d, h, value)
                refs["XS"][d * 3 + n, at, :] = value[0:8]
                rows.append(value[8:9])
            refs["X8"][n, at, :] = stacked_rows(rows)


def second_pair(refs, p):
    SS, KS, K8 = refs["SS"], refs["KS"], refs["K8"]
    total, total8 = {}, {}
    for e in range(2):
        high = refs["U2H"][p, e : e + 2].reshape(192, 256)
        low = refs["U2L"][p, e : e + 2].reshape(192, 256)
        scale = [SS[e + 1, 0], jnp.where(row_of(SS[e + 1, 1]) == 0, 0.0, SS[e + 1, 1])]
        for a in range(2):
            n = e + a
            force = forces(refs, a, high, low)
            for h in range(2):
                for q in range(2):
                    for b in range(2):
                        for d in range(3):
                            add_to(total, (n, d, q, h), scale[b] * block_of(force, b, q, d, h))
                    add_to(total8, (n, q, h), SS[e + 1, 3] * block8_of(force, 1, q, h))
    for h in range(2):
        at = pl.ds(pl.multiple_of((COLS + 2 * p + h) * 8, 8), 8)
        for n in range(3):
            K8[n, at, :] = total8[n, 0, h] + to_next_z(total8[n, 1, h])
            for d in range(3):
                KS[d * 3 + n, at, :] = total[n, d, 0, h] + to_next_z(total[n, d, 1, h])


def put_halves(ref, row, rows_low, lanes, value):
    high, low = halves(value)
    ref[row : row + WIDE, lanes] = high
    ref[rows_low + row : rows_low + row + WIDE, lanes] = low


def all_to_all_rows(left, right):
    return lax.dot_general(left, right, (((1,), (1,)), ((), ())), preferred_element_type=F32)


def gram_sums(refs):
    XS, KS, X8, K8, LM = refs["XS"], refs["KS"], refs["X8"], refs["K8"], refs["LM"]
    GX, GY = refs["GX"], refs["GY"]
    GY[...] = jnp.zeros(GY.shape, BF16)

    def folded(width):
        out = all_to_all_rows(GX[:, 0:width], GY[:, 0:width])
        rows = out[0:WIDE] + out[WIDE : 2 * WIDE]
        return rows[:, 0:128] + rows[:, 128:256]

    def own(i, total):
        d, n = i // 2, i % 2
        for y in range(8):
            lanes = slice(y * 128, y * 128 + 128)
            rows = pl.ds(y, WIDE, stride=8)
            value = XS[d * 3 + n, rows, :]
            put_halves(GX, 0, WIDE, lanes, value)
            put_halves(GY, 0, 128, lanes, KS[d * 3 + n, rows, :])
            put_halves(GY, WIDE, 128, lanes, value * LM[n, 0, y : y + 1])
        return total + folded(1024)

    total = lax.fori_loop(0, 6, own, jnp.zeros((WIDE, 128), F32))
    GY[...] = jnp.zeros(GY.shape, BF16)

    def rim(d, total):
        for y in range(8):
            lanes = slice(y * 128, y * 128 + 128)
            rows = pl.ds(y, WIDE, stride=8)
            put_halves(GX, 0, WIDE, lanes, XS[d * 3 + 2, rows, :])
            put_halves(GY, 0, 128, lanes, KS[d * 3 + 2, rows, :])
        return total + folded(1024)

    total = lax.fori_loop(0, 3, rim, total)
    for n in range(3):
        for d in range(3):
            lanes = slice((n * 3 + d) * 128, (n * 3 + d) * 128 + 128)
            rows = pl.ds(d, WIDE, stride=8)
            put_halves(GX, 0, WIDE, lanes, X8[n, rows, :])
            put_halves(GY, 0, 128, lanes, K8[n, rows, :])
    refs["pay"][...] = total + folded(1152)


def compute(refs):
    prepare_fields(refs)

    def one(p, carry):
        current_pair(refs, p)
        previous_pair(refs, p)
        return carry

    lax.fori_loop(0, PAIRS, one, 0)

    def two(p, carry):
        second_pair(refs, p)
        return carry

    lax.fori_loop(0, 3 * PAIRS, two, 0)
    gram_sums(refs)


def compute_kernel(names, *args):
    compute(dict(zip(names, args)))


COMPUTE_SCRATCH = {
    "SS": ((4, 4, 8, 128), F32),
    "LM": ((3, 2, 8, 128), F32),
    "PM": ((3, 3, 8, 128), F32),
    "P8": ((3, 8, 128), F32),
    "VV": ((2, 3, 2, 5, 16, 128), F32),
    "UH": ((5, 96, 256), BF16),
    "UL": ((5, 96, 256), BF16),
    "U2H": ((3 * PAIRS, 3, 96, 256), BF16),
    "U2L": ((3 * PAIRS, 3, 96, 256), BF16),
    "XS": ((9, WIDE * 8, 128), F32),
    "KS": ((9, WIDE * 8, 128), F32),
    "X8": ((3, WIDE * 8, 128), F32),
    "K8": ((3, WIDE * 8, 128), F32),
    "GX": ((2 * WIDE, 1152), BF16),
    "GY": ((256, 1152), BF16),
}


def reduce_groups(sizes):
    nx, ny = sizes
    near = min(4, nx)
    groups = [("bx", 1, near), ("bx", near, nx // near), ("by", 1, ny)]
    return [g for g in groups if g[2] > 1]


def peers_of(axis, stride, size):
    at = lax.axis_index(axis)
    place = (at // stride) % size
    base = at - place * stride
    return place, [(lax.rem(place + k, size), base + lax.rem(place + k, size) * stride) for k in range(1, size)]


def greet_reducers(sizes, barrier):
    count = 0
    for axis, stride, size in reduce_groups(sizes):
        for _, peer in peers_of(axis, stride, size)[1]:
            pl.semaphore_signal(barrier, inc=1, device_id={axis: peer}, device_id_type=MESH)
            count += 1
    pl.semaphore_signal(
        barrier, inc=1, device_id={"real": 1 - lax.axis_index("real")}, device_id_type=MESH
    )
    return count + 1


def reduce_and_finish(sizes, dofs, refs):
    groups = reduce_groups(sizes)
    value = refs["pay"][...]
    for i, (axis, stride, size) in enumerate(groups):
        slots = refs[f"slots{i}"]
        place, peers = peers_of(axis, stride, size)
        slots[place] = value
        copies = []
        for k, (there, peer) in enumerate(peers):
            copies.append(
                pltpu.make_async_remote_copy(
                    src_ref=slots.at[place],
                    dst_ref=slots.at[place],
                    send_sem=refs[f"rsend{i}"].at[k],
                    recv_sem=refs[f"rrecv{i}"].at[place],
                    device_id={axis: peer},
                    device_id_type=MESH,
                )
            )
        for copy in copies:
            copy.start()
        for there, peer in peers:
            pltpu.make_async_remote_copy(
                src_ref=slots.at[place],
                dst_ref=slots.at[there],
                send_sem=refs[f"rsend{i}"].at[0],
                recv_sem=refs[f"rrecv{i}"].at[there],
                device_id={axis: peer},
                device_id_type=MESH,
            ).wait_recv()
        value = slots[0]
        for k in range(1, size):
            value = value + slots[k]
        for copy in copies:
            copy.wait_send()
    value = value / dofs
    stiff, mass = value, pltpu.roll(value, 128 - WIDE, 1)
    lane, row = lane_of(value), row_of(value)
    diagonal = (lane == row) & (row < COLS)
    stiff_diag = jnp.where(diagonal, stiff, 0.0)
    mass_diag = jnp.where(diagonal, mass, 0.0)
    quotient_col = jnp.sum(stiff_diag, axis=1, keepdims=True) / jnp.sum(
        jnp.where(diagonal, mass, jnp.where((lane == 0) & (row >= COLS), 1.0, 0.0)),
        axis=1,
        keepdims=True,
    )
    denominator_col = jnp.sum(mass_diag, axis=1, keepdims=True)
    quotient_row = jnp.sum(
        jnp.where((lane == row) & (row < COLS), quotient_col, 0.0), axis=0, keepdims=True
    )
    shifted_row = pltpu.roll(jnp.broadcast_to(quotient_row, (8, 128)), COLS, 1)[0:1]
    wide_col = jnp.broadcast_to(quotient_col, (WIDE, 128))
    shifted_col = pltpu.roll(wide_col, COLS, 0)
    for name, gram in (("gram_stiff", stiff), ("gram_mass", mass)):
        moved = pltpu.roll(gram, 128 - COLS, 1)
        side = jnp.where(
            lane < COLS, gram, jnp.where(lane < 2 * COLS, gram - shifted_row * moved, moved)
        )
        moved = pltpu.roll(side, WIDE - COLS, 0)
        full = jnp.where(
            row < COLS, side, jnp.where(row < 2 * COLS, side - shifted_col * moved, moved)
        )
        refs[name][0] = full[0 : 3 * COLS, 0 : 3 * COLS]
    weights, power_sum = [], jnp.zeros((1, 1), F32)
    for j in range(COLS):
        quotient = quotient_col[j : j + 1, 0:1]
        inverse = 1.0 / quotient
        square = inverse * inverse
        powered = square * square
        power_sum = power_sum + powered
        weights.append((quotient, powered / denominator_col[j : j + 1, 0:1]))
    terms = refs["terms"]
    for n in range(2):
        stiff_sum = jnp.zeros((8, 128), F32)
        mass_sum = jnp.zeros((8, 128), F32)
        for j, (quotient, weight) in enumerate(weights):
            stiff_sum = stiff_sum + weight * refs["ES"][j, n]
            mass_sum = mass_sum + (weight * quotient) * refs["EM"][j, n]
        terms[0, n] = (
            3.0 * refs["FE"][0, 0, n + 1, 0:8] * stiff_sum
            - refs["FE"][0, 1, n + 1, 0:8] * mass_sum
        )
    terms[0, 2] = jnp.broadcast_to(power_sum, (8, 128))
    real = lax.axis_index("real")
    swap = pltpu.make_async_remote_copy(
        src_ref=terms.at[0],
        dst_ref=terms.at[1],
        send_sem=refs["swap_sem"].at[0],
        recv_sem=refs["swap_sem"].at[1],
        device_id={"real": 1 - real},
        device_id_type=MESH,
    )
    swap.start()
    for j, (quotient, _) in enumerate(weights):
        for d in range(3):
            for n in range(2):
                refs["search"][0, j, d, n] = refs["first"][j, d, n] - quotient * refs["second"][j, d, n]
    swap.wait()
    overall = terms[0, 2] + terms[1, 2]
    for n in range(2):
        whole = (terms[0, n] + terms[1, n]) / overall
        upper = pltpu.roll(whole, 64, 1)
        refs["sens"][n] = jnp.where(real == 0, whole, upper)[:, 0:64]


def finish_kernel(sizes, dofs, names, *args):
    refs = dict(zip(names, args))
    barrier = pltpu.get_barrier_semaphore()
    count = greet_reducers(sizes, barrier)
    pl.semaphore_wait(barrier, count)
    reduce_and_finish(sizes, dofs, refs)


def reduce_scratch(sizes):
    out = {}
    for i, (_, _, size) in enumerate(reduce_groups(sizes)):
        out[f"slots{i}"] = pltpu.VMEM((size, WIDE, 128), F32)
        out[f"rsend{i}"] = pltpu.SemaphoreType.DMA((size,))
        out[f"rrecv{i}"] = pltpu.SemaphoreType.DMA((size,))
    out["terms"] = pltpu.VMEM((2, 3, 8, 128), F32)
    out["swap_sem"] = pltpu.SemaphoreType.DMA((2,))
    return out


VMEM_SPEC = pl.BlockSpec(memory_space=pltpu.VMEM)
ANY_SPEC = pl.BlockSpec(memory_space=pl.ANY)


def run(kernel, statics, ins, outs, scratch, specs=None, collective_id=None):
    names = [*ins, *outs, *scratch]
    params = dict(vmem_limit_bytes=60 * 2**20)
    if collective_id is not None:
        params.update(collective_id=collective_id, has_side_effects=True)
    result = pl.pallas_call(
        functools.partial(kernel, *statics, names),
        out_shape=[jax.ShapeDtypeStruct(shape, dtype) for shape, dtype in outs.values()],
        in_specs=[(specs or {}).get(name, VMEM_SPEC) for name in ins],
        out_specs=[VMEM_SPEC for _ in outs],
        scratch_shapes=list(scratch.values()),
        compiler_params=pltpu.CompilerParams(**params),
        name=kernel.__name__,
    )(*ins.values())
    return dict(zip(outs, result))


def shards(sizes, current, previous, element_stiffness, preconditioner, modulus, density, solid, clamped):
    size_x, size_y, size_z = modulus.shape
    nx, ny = sizes
    dofs = 3.0 * size_x * size_y * size_z * nx * ny
    bottom = (jnp.arange(size_z) == 0).astype(F32)
    keep = 1.0 - clamped.astype(F32)[:, :, None] * bottom
    share = solid[0].astype(F32)
    fields = jnp.stack(
        [
            modulus * (0.02 + 0.98 * share),
            density * (0.1 + 0.9 * share),
            keep,
            preconditioner[0, 0],
            preconditioner[0, 1],
            preconditioner[0, 2],
        ],
        0,
    ).reshape(2, 3, size_x, size_y, size_z)
    pick_row, pick_col, allow = operator_tables()
    halo = run(
        halo_kernel,
        (sizes,),
        dict(
            cur=current[0],
            prev=previous[0],
            fld=fields,
            elem=element_stiffness,
            pick_row=jnp.asarray(pick_row),
            pick_col=jnp.asarray(pick_col),
            allow=jnp.asarray(allow),
        ),
        dict(
            XC=((COLS, 3, 5, 16, 128), F32),
            XP=((COLS, 3, 3, 16, 128), F32),
            FE=((2, 3, 5, 16, 128), F32),
            WH=((2, 128, 192), BF16),
            WL=((2, 128, 192), BF16),
        ),
        dict(
            send_sem=pltpu.SemaphoreType.DMA((N_HALO,)),
            recv_sem=pltpu.SemaphoreType.DMA((N_HALO,)),
            local_sem=pltpu.SemaphoreType.DMA((3,)),
        ),
        specs=dict(cur=ANY_SPEC, prev=ANY_SPEC, fld=ANY_SPEC),
        collective_id=1,
    )
    local = run(
        compute_kernel,
        (),
        halo,
        dict(
            pay=((WIDE, 128), F32),
            first=((COLS, 3, 2, 8, 128), F32),
            second=((COLS, 3, 2, 8, 128), F32),
            ES=((COLS, 2, 8, 128), F32),
            EM=((COLS, 2, 8, 128), F32),
        ),
        {name: pltpu.VMEM(shape, dtype) for name, (shape, dtype) in COMPUTE_SCRATCH.items()},
    )
    done = run(
        finish_kernel,
        (sizes, dofs),
        dict(**local, FE=halo["FE"]),
        dict(
            gram_stiff=((1, 3 * COLS, 3 * COLS), F32),
            gram_mass=((1, 3 * COLS, 3 * COLS), F32),
            search=((1, COLS, 3, 2, 8, 128), F32),
            sens=((2, 8, 64), F32),
        ),
        reduce_scratch(sizes),
        collective_id=2,
    )
    return done["gram_stiff"], done["gram_mass"], done["search"], done["sens"]


def solution(mesh):
    sizes = (mesh.shape["bx"], mesh.shape["by"])
    return jax.shard_map(
        functools.partial(shards, sizes),
        mesh=mesh,
        in_specs=(
            P("real", None, None, "bx", "by", None),
            P("real", None, None, "bx", "by", None),
            P(),
            P("real", None, "bx", "by", None),
            P("bx", "by", None),
            P("bx", "by", None),
            P("real", "bx", "by", None),
            P("bx", "by"),
        ),
        out_specs=(
            P("real", None, None),
            P("real", None, None),
            P("real", None, None, "bx", "by", None),
            P("bx", "by", "real"),
        ),
        check_vma=False,
    )
```

time: 273 us -> 75.8 us (0.28)
  blocking collectives: 72.8 us -> 0 us
  local copies, waits for them, and re-layouts: 74.3 us -> 8.4 us
  Pallas kernels: 0 us -> 64 us
  starting transfers between devices: 46.1 us -> 0 us
  matrix products: 34 us -> 0 us
  other arithmetic: 29.4 us -> 2.2 us
  waiting for transfers between devices: 11.4 us -> 0 us
    psum x4 -> x0, blocking collectives: 67.9 us -> none  [over_axes(): return functools.reduce(lax.psum, axes, array)]
    pallas_call x0 -> x3, Pallas kernels: none -> 64 us  [run(): pl.pallas_call(functools.partial(kernel, *statics, names), out_shape=[jax...]
    ppermute x10 -> x0, starting transfers between devices: 40.9 us -> none  [from_behind(): lax.ppermute(value, axis, [(source, source + steps) for source in range(l...]
    another operation x122 -> x1, local copies, waits for them, and re-layouts: 37 us -> 0.7 us  [shards(): jnp.stack([modulus * (0.02 + 0.98 * share), density * (0.1 + 0.9 * share)...]
    dot_general x50 -> x0, matrix products: 34 us -> none  [the longest x32 22.5 us: gram_matrix(): jnp.einsum('ik,jk->ij', flat_left, right_block.reshape(right_block.shape[...]
    dynamic_update_slice x18 -> x0, other arithmetic: 18.2 us -> none  [grouped_pass(): assembled, energy_stiff, energy_mass = lax.map(run_group, groups)]
    squeeze x60 -> x0, local copies, waits for them, and re-layouts: 14 us -> none  [the longest x12 13.2 us: grouped_pass(): assembled, energy_stiff, energy_mass = lax.map(run_group, groups)]
    ppermute x10 -> x0, waiting for transfers between devices: 11.4 us -> none  [from_behind(): lax.ppermute(value, axis, [(source, source + steps) for source in range(l...]
  transfers between devices with their start and end apart: 11 -> 0, of which waited for: 5 -> 0; matrix products, arithmetic and copies ran while one was open for 7% -> 0% of each run, Pallas kernels for 0% -> 0%
where the time goes in v1:
time: 75.8 us; the launch traced here: 75.2 us
  Pallas kernels  64 us (84%)
  local copies, waits for them, and re-layouts  8.4 us (11%)
  other arithmetic  2.2 us (3%)
    pallas_call x3, Pallas kernels, run(): pl.pallas_call(functools.partial(kernel, *statics, names), out_shape=[jax...  64 us
    unnamed x6, local copies, waits for them, and re-layouts  5 us
    pallas_call x2, local copies, waits for them, and re-layouts, run(): pl.pallas_call(functools.partial(kernel, *statics, names), out_shape=[jax...  2.7 us

profile of v1, /device:TPU:2, one launch (start us, length us, event | category | flops | bytes accessed | tf_op | source)
XLA Modules:
  0.0 75.2 jit_solution(17259336213545657760)
XLA Ops:
  0.6 0.7 convert_element_type.15
  1.3 0.7 constant_dynamic-update-slice_fusion.5
  2.0 0.7 constant_dynamic-update-slice_fusion.4
  2.8 0.1 constant_dynamic-update-slice_fusion.3
  2.8 0.7 constant_dynamic-update-slice_fusion.2
  3.5 0.7 constant_dynamic-update-slice_fusion.1
  4.2 0.7 constant_dynamic-update-slice_fusion
  4.9 0.0 copy-start
  4.9 0.6 copy-done
  5.6 13.6 %halo_kernel.1 = (f32[12,3,5,16,128]{4,3,2,1,0:T(8,128)}, f32[12,3,3,16,128]{4,3,2,1,0:T(8,128)}, f32[2,3,5,16,128]{4,3,2,1,0:T(8,128)}, bf16[2,128,192]{2,1,0:T(8,128)(2,1)}, bf16[2,128,192]{2,1,0:T(8,128)(2,1)}) custom-call(f32[12,3,2,8,128]{4,3,2,1,0:T(8,128)} %bitcast.21, f32[12,3,2,8,128]{4,3,2,1,0:T(8,128)} %bitcast.22, f32[2,3,2,8,128]{4,3,2,1,0:T(8,128)} %bitcast.23, ...), custom_call_target="tpu_custom_call" | custom-call | tf_op jit(solution)/shard_map/halo_kernel/pallas_call | solution.py:636
  19.1 18.7 %compute_kernel.1 = (f32[48,128]{1,0:T(8,128)}, f32[12,3,2,8,128]{4,3,2,1,0:T(8,128)}, f32[12,3,2,8,128]{4,3,2,1,0:T(8,128)}, f32[12,2,8,128]{3,2,1,0:T(8,128)}, f32[12,2,8,128]{3,2,1,0:T(8,128)}) custom-call(f32[12,3,5,16,128]{4,3,2,1,0:T(8,128)} %get-tuple-element.14.args_0_, f32[12,3,3,16,128]{4,3,2,1,0:T(8,128)} %get-tuple-element.15.args_1_, ...), custom_call_target="tpu_custom_call" | custom-call | tf_op jit(solution)/shard_map/compute_kernel/pallas_call | solution.py:636
  37.8 31.7 %finish_kernel.1 = (f32[1,36,36]{2,1,0:T(8,128)}, f32[1,36,36]{2,1,0:T(8,128)}, f32[1,12,3,2,8,128]{5,4,3,2,1,0:T(8,128)}, f32[2,8,64]{2,1,0:T(8,128)}) custom-call(f32[48,128]{1,0:T(8,128)} %get-tuple-element.19.args_0_, f32[12,3,2,8,128]{4,3,2,1,0:T(8,128)} %get-tuple-element.20.args_1_, f32[12,3,2,8,128]{4,3,2,1,0:T(8,128)} %get-tuple-element.21.args_2_, ...), custom_call_target="tpu_custom_call" | custom-call | tf_op jit(solution)/shard_map/finish_kernel/pallas_call | solution.py:636
  69.5 1.4 %copy.15 = f32[1,36,36]{2,0,1:T(1,128)} copy(f32[1,36,36]{2,1,0:T(8,128)} %get-tuple-element.24) | data formatting | bytes 10368 | tf_op jit(solution)/shard_map/finish_kernel/pallas_call | solution.py:636
  70.9 1.4 %copy.16 = f32[1,36,36]{2,0,1:T(1,128)} copy(f32[1,36,36]{2,1,0:T(8,128)} %get-tuple-element.25) | data formatting | bytes 10368 | tf_op jit(solution)/shard_map/finish_kernel/pallas_call | solution.py:636
  72.2 1.7 %copy.24 = f32[1,12,3,2,8,128]{5,4,3,2,1,0:T(8,128)} copy(f32[1,12,3,2,8,128]{5,4,3,2,1,0:T(8,128)} %get-tuple-element.34) | data formatting | bytes 589824
  73.9 1.3 %copy.25 = f32[2,8,64]{2,1,0:T(8,128)} copy(f32[2,8,64]{2,1,0:T(8,128)} %get-tuple-element.35) | data formatting | bytes 8192
  (1 shorter events, 0.0 us)
Async XLA Ops:
  4.9 0.6 copy-start

commit v2 on v1

v2 whole, which is shorter than its diff:
```python
import functools

import jax
import jax.numpy as jnp
import numpy as np
from jax import lax
from jax.experimental import pallas as pl
from jax.experimental.pallas import tpu as pltpu
from jax.sharding import PartitionSpec as P

MESH = pl.DeviceIdType.MESH
F32 = jnp.float32
BF16 = jnp.bfloat16
COLS = 12
WIDE = 4 * COLS
PAIRS = COLS // 2
CHUNKS = 3
PER_CHUNK = COLS // CHUNKS
NOWHERE = 1000.0
DIRS = [
    (1, 0, (0, 2), (0, 8), 3, 0),
    (-1, 0, (1, 1), (0, 8), 0, 0),
    (1, 1, (0, 2), (0, 2), 3, 8),
    (1, -1, (0, 2), (7, 1), 3, 10),
    (-1, 1, (1, 1), (0, 2), 0, 8),
    (-1, -1, (1, 1), (7, 1), 0, 10),
    (0, 1, (0, 2), (0, 2), 1, 8),
    (0, -1, (0, 2), (7, 1), 1, 10),
]
PREV_DIRS = [
    (1, 0, (0, 1), (0, 8), 2, 0),
    (1, 1, (0, 1), (0, 1), 2, 8),
    (0, 1, (0, 2), (0, 1), 0, 8),
]
N_DIRS = len(DIRS)
N_HALO = N_DIRS * (1 + CHUNKS) + len(PREV_DIRS)


def operator_tables():
    out = []
    for bits in ((0, 1), (1,)):
        half = 96 + 16 * len(bits)
        pick_row = np.zeros((2 * half, 25), np.float32)
        pick_row[:, 24] = -NOWHERE
        for a in range(2):
            for b in range(2):
                for q in range(2):
                    for d in range(3):
                        i = 3 * (4 * a + 2 * b + q) + d
                        for y in range(8):
                            m = a * half + ((b * 2 + q) * 3 + d) * 8 + y
                            pick_row[m, i], pick_row[m, 24] = 1, y - b
                        if b in bits:
                            m = a * half + 96 + (bits.index(b) * 2 + q) * 8 + d
                            pick_row[m, i], pick_row[m, 24] = 1, 8 - b
        out.append(pick_row)
    first, second = [], []
    for a in range(2):
        for d in range(3):
            for q in range(2):
                for row in range(16):
                    first.append((a, d, q, -1 if row == 10 else row if row < 10 else None))
        for planes in ([(0, 0), (1, 0)], [(0, 1), (1, 1)], [(2, 0), (2, 1)]):
            for d, q in planes:
                second += [(a, d, q, y) for y in range(8)]
        for q in range(2):
            second += [(a, d % 3, q, 8 if d < 3 else None) for d in range(8)]
    for rows in (first, second):
        size = 3 * len(rows)
        pick_col = np.zeros((24, 2 * size), np.float32)
        row_y = np.full((8, size), NOWHERE * 2, np.float32)
        for part in range(3):
            for k, (a, d, q, y) in enumerate(rows):
                if y is None:
                    continue
                at = part * len(rows) + k
                row_y[:, at] = y
                for b in range(2):
                    pick_col[3 * (4 * a + 2 * b + q) + d, b * size + at] = 1
        out += [pick_col, row_y]
    row1, row2, col1, y1, col2, y2 = out
    tables = dict(
        rows=np.concatenate([row1, row2]), cols=np.concatenate([col1, col2], 1), ys=np.concatenate([y1, y2], 1)
    )
    return tables


def exact_dot(left, right):
    return lax.dot_general(
        left,
        right,
        (((1,), (0,)), ((), ())),
        preferred_element_type=F32,
        precision=lax.Precision.HIGHEST,
    )


def halves(value):
    high = value.astype(BF16)
    return high, (value - high.astype(F32)).astype(BF16)


def lane_of(value):
    return lax.broadcasted_iota(jnp.int32, value.shape, 1)


def row_of(value):
    return lax.broadcasted_iota(jnp.int32, value.shape, 0)


def from_next_z(value):
    return jnp.where(lane_of(value) == 127, 0.0, pltpu.roll(value, 127, 1))


def to_next_z(value):
    return jnp.where(lane_of(value) == 0, 0.0, pltpu.roll(value, 1, 1))


def spread(row):
    return jnp.broadcast_to(row, (8, 128))


def from_lower_y(main, below):
    return jnp.where(row_of(main) == 0, spread(below), pltpu.roll(main, 1, 0))


def from_upper_y(main, above):
    return jnp.where(row_of(main) == 7, spread(above), pltpu.roll(main, 7, 0))


def stacked_rows(rows):
    out = jnp.zeros((8, 128), F32)
    at = row_of(out)
    for d, row in enumerate(rows):
        out = jnp.where(at == d, spread(row), out)
    return out


def column_rows(index):
    return pl.ds(pl.multiple_of(index * 8, 8), 8)


class Halo:
    def __init__(self, sizes, refs):
        self.refs = refs
        self.bx, self.by = lax.axis_index("bx"), lax.axis_index("by")
        self.nx, self.ny = sizes

    def inside(self, dx, dy):
        x, y = self.bx + dx, self.by + dy
        return (x >= 0) & (x < self.nx) & (y >= 0) & (y < self.ny)

    def copy(self, source, target, job, at):
        dx, dy, (x0, xn), (y0, yn), tx, ty = job
        return pltpu.make_async_remote_copy(
            src_ref=source.at[:, :, x0 : x0 + xn, y0 : y0 + yn, :],
            dst_ref=target.at[:, :, tx : tx + xn, ty : ty + yn, :],
            send_sem=self.refs["send_sem"].at[at],
            recv_sem=self.refs["recv_sem"].at[at],
            device_id={"bx": self.bx - dx, "by": self.by - dy},
            device_id_type=MESH,
        )

    def fields(self):
        FE = self.refs["FE"]
        own = FE.at[:, :, 1:3, 0:8, :]
        return [(job, self.copy(own, FE, job, k)) for k, job in enumerate(DIRS)]

    def chunk(self, c):
        part = pl.ds(c * PER_CHUNK, PER_CHUNK)
        source, target = self.refs["cur"].at[part], self.refs["XC"].at[part]
        return [
            (job, self.copy(source, target, job, (c + 1) * N_DIRS + k))
            for k, job in enumerate(DIRS)
        ]

    def previous(self):
        first = N_DIRS * (1 + CHUNKS)
        return [
            (job, self.copy(self.refs["prev"], self.refs["XP"], job, first + k))
            for k, job in enumerate(PREV_DIRS)
        ]

    def start(self, copies):
        for job, copy in copies:
            pl.when(self.inside(-job[0], -job[1]))(copy.start)

    def arrived(self, copies):
        for job, copy in copies:
            pl.when(self.inside(job[0], job[1]))(copy.wait_recv)

    def left(self, copies):
        for job, copy in copies:
            pl.when(self.inside(-job[0], -job[1]))(copy.wait_send)

    def greet(self, barrier):
        count = 0
        for dx in (-1, 0, 1):
            for dy in (-1, 0, 1):
                if dx == 0 and dy == 0:
                    continue
                there = self.inside(dx, dy)

                @pl.when(there)
                def _():
                    pl.semaphore_signal(
                        barrier,
                        inc=1,
                        device_id={"bx": self.bx + dx, "by": self.by + dy},
                        device_id_type=MESH,
                    )

                count = count + there.astype(jnp.int32)
        return count


def own_fields(refs):
    FE = refs["FE"]
    shape = (8, 128)
    lane = lax.broadcasted_iota(jnp.int32, shape, 1)
    row = lax.broadcasted_iota(jnp.int32, shape, 0)
    for x in range(2):
        share = refs["solid_in"][x].astype(F32)
        FE[0, 0, x + 1, 0:8] = refs["modulus_in"][x] * (0.02 + 0.98 * share)
        FE[0, 1, x + 1, 0:8] = refs["density_in"][x] * (0.1 + 0.9 * share)
        held = jnp.broadcast_to(refs["clamped_in"][x : x + 1].astype(F32), (8, 8))
        held = jnp.where(
            lax.broadcasted_iota(jnp.int32, (8, 8), 0) == lax.broadcasted_iota(jnp.int32, (8, 8), 1),
            held,
            0.0,
        )
        held = jnp.sum(held, axis=1, keepdims=True)
        FE[0, 2, x + 1, 0:8] = 1.0 - jnp.where(lane == 0, held, 0.0)


def build_operators(refs):
    for row, rows, at, out in ((0, 256, 0, "W1"), (256, 224, 576, "W2")):
        table = refs["rows_in"][row : row + rows]
        size = refs[out].shape[1]
        both = exact_dot(
            exact_dot(table[:, 0:24], refs["elem_in"][...]),
            refs["cols_in"][:, 2 * at : 2 * (at + size)],
        )
        gap = refs["ys_in"][0:1, at : at + size] - table[:, 24:25]
        full = jnp.where(gap == 0.0, both[:, 0:size], 0.0) + jnp.where(
            gap == 1.0, both[:, size : 2 * size], 0.0
        )
        high = full.astype(BF16).astype(F32)
        refs[out][...] = jnp.where(lane_of(full) < 2 * size // 3, high, full - high).astype(BF16)


def prepare_fields(refs):
    FE, SS, LM, PM, P8 = refs["FE"], refs["SS"], refs["LM"], refs["PM"], refs["P8"]
    mass_sum = []
    for e in range(4):
        for kind in range(2):
            main, row8 = FE[0, kind, e, 0:8], FE[0, kind, e, 8:9]
            below = FE[0, kind, e, 10:11]
            lower = from_lower_y(main, below)
            here8, lower8 = spread(row8), spread(main[7:8])
            if kind == 0:
                SS[e, 0], SS[e, 1], SS[e, 2], SS[e, 3] = main, lower, here8, lower8
                SS[e, 4] = jnp.where(row_of(lower) == 0, 0.0, lower)
            else:
                mass_sum.append((main + lower, here8 + lower8))
    for n in range(3):
        for part in range(2):
            total = mass_sum[n][part] + mass_sum[n + 1][part]
            keep = FE[0, 2, n + 1, 0:8] if part == 0 else spread(FE[0, 2, n + 1, 8:9])
            LM[n, part] = (total + to_next_z(total)) * 0.125 * keep
        for d in range(3):
            PM[n, d] = FE[1, d, n + 1, 0:8] * FE[0, 2, n + 1, 0:8]
        P8[n] = stacked_rows([FE[1, d, n + 1, 8:9] * FE[0, 2, n + 1, 8:9] for d in range(3)])


def forces(weights, high, low):
    stacked = jnp.concatenate([high, low, high], 0)
    return lax.dot_general(
        weights, stacked, (((1,), (0,)), ((), ())), preferred_element_type=F32
    )


def block_of(force, row, h):
    return force[row : row + 8, h * 128 : h * 128 + 128]


def add_to(store, key, value):
    store[key] = value if key not in store else store[key] + value


def store_halves(high_ref, low_ref, lead, row, h, value):
    high, low = halves(value)
    at = (*lead, slice(row, row + 16), slice(h * 128, h * 128 + 128))
    high_ref[at] = high
    low_ref[at] = low


def store_second(refs, lead, h, planes, edge):
    moved = [from_next_z(plane) for plane in planes]
    blocks = [
        (planes[0], planes[1]),
        (moved[0], moved[1]),
        (planes[2], moved[2]),
        (edge, from_next_z(edge)),
    ]
    for k, block in enumerate(blocks):
        store_halves(refs["U2H"], refs["U2L"], lead, k * 16, h, jnp.concatenate(block, 0))


def current_pair(refs, p):
    XC, FE, VV, UH, UL = refs["XC"], refs["FE"], refs["VV"], refs["UH"], refs["UL"]
    SS, LM, PM, P8 = refs["SS"], refs["LM"], refs["PM"], refs["P8"]
    XS, KS, X8, K8 = refs["XS"], refs["KS"], refs["X8"], refs["K8"]
    edge = {}
    for h in range(2):
        for x in range(5):
            keep = FE[0, 2, x]
            rows = []
            for d in range(3):
                value = XC[2 * p + h, d, x] * keep
                moved = from_next_z(value)
                store_halves(UH, UL, (x,), (d * 2) * 16, h, value)
                store_halves(UH, UL, (x,), (d * 2 + 1) * 16, h, moved)
                if 1 <= x <= 3:
                    VV[h, d, 0, x - 1] = value
                    VV[h, d, 1, x - 1] = moved
                rows.append(value[8:9])
            if 1 <= x <= 3:
                edge[h, 0, x] = stacked_rows(rows)
                edge[h, 1, x] = from_next_z(edge[h, 0, x])
    total, total8, energy, energy8 = {}, {}, {}, {}
    for e in range(4):
        high = UH[e : e + 2].reshape(192, 256)
        low = UL[e : e + 2].reshape(192, 256)
        used = [a for a in range(2) if 0 <= e - 1 + a <= 2]
        force = forces(refs["W1"][used[0] * 128 : used[-1] * 128 + 128, :], high, low)
        for a in used:
            n = e - 1 + a
            start = (a - used[0]) * 128
            for h in range(2):
                for b in range(2):
                    for q in range(2):
                        for d in range(3):
                            block = block_of(force, start + ((b * 2 + q) * 3 + d) * 8, h)
                            add_to(total, (n, d, q, h), SS[e, b] * block)
                            if e in (1, 2):
                                add_to(energy, (e, b, h), VV[h, d, q, e + a - 1, 0:8] * block)
                        block = block_of(force, start + 96 + (b * 2 + q) * 8, h)
                        add_to(total8, (n, q, h), SS[e, 2 + b] * block)
                        if e in (1, 2) and b == 1:
                            add_to(energy8, (e, h), edge[h, q, e + a] * block)
    zero = jnp.zeros((8, 128), F32)
    for h in range(2):
        c = 2 * p + h
        for n in range(3):
            stiff8 = total8[n, 0, h] + to_next_z(total8[n, 1, h])
            first8 = P8[n] * stiff8
            second8 = P8[n] * LM[n, 1] * edge[h, 0, n + 1]
            for ref, col, value in (
                (X8, 0, edge[h, 0, n + 1]),
                (X8, 1, first8),
                (X8, 2, second8),
                (K8, 0, zero),
            ):
                ref[n, column_rows(col * COLS + c), :] = value
            firsts, seconds = [], []
            for d in range(3):
                stiff = total[n, d, 0, h] + to_next_z(total[n, d, 1, h])
                here = VV[h, d, 0, n, 0:8]
                firsts.append(PM[n, d] * stiff)
                seconds.append(PM[n, d] * LM[n, 0] * here)
                for ref, col, value in (
                    (XS, 0, here),
                    (XS, 1, firsts[d]),
                    (XS, 2, seconds[d]),
                    (KS, 0, stiff if n < 2 else zero),
                ):
                    ref[d * 3 + n, column_rows(col * COLS + c), :] = value
                if n < 2:
                    refs["first"][c, d, n] = firsts[d]
                    refs["second"][c, d, n] = seconds[d]
            store_second(refs, (p, n), h, firsts, first8)
            store_second(refs, (PAIRS + p, n), h, seconds, second8)
        for e in (1, 2):
            above = jnp.sum(energy8[e, h], axis=0, keepdims=True)
            refs["ES"][c, e - 1] = energy[e, 0, h] + from_upper_y(energy[e, 1, h], above)
            square = 0.0
            for x in (e - 1, e):
                for d in range(3):
                    for q in range(2):
                        square = square + VV[h, d, q, x] * VV[h, d, q, x]
            main = square[0:8]
            refs["EM"][c, e - 1] = (main + from_upper_y(main, square[8:9])) * 0.125


def previous_pair(refs, p):
    for h in range(2):
        c = 2 * p + h
        at = column_rows(3 * COLS + c)
        for n in range(3):
            rows, planes = [], []
            for d in range(3):
                value = refs["XP"][c, d, n] * refs["FE"][0, 2, n + 1]
                planes.append(value[0:8])
                refs["XS"][d * 3 + n, at, :] = planes[d]
                rows.append(value[8:9])
            edge = stacked_rows(rows)
            refs["X8"][n, at, :] = edge
            store_second(refs, (2 * PAIRS + p, n), h, planes, edge)


def second_pair(refs, p):
    SS, KS, K8 = refs["SS"], refs["KS"], refs["K8"]
    total, total8 = {}, {}
    for e in range(2):
        high = refs["U2H"][p, e : e + 2].reshape(128, 256)
        low = refs["U2L"][p, e : e + 2].reshape(128, 256)
        force = forces(refs["W2"][...], high, low)
        for a in range(2):
            n = e + a
            for h in range(2):
                for q in range(2):
                    for b in range(2):
                        for d in range(3):
                            block = block_of(force, a * 112 + ((b * 2 + q) * 3 + d) * 8, h)
                            add_to(total, (n, d, q, h), SS[e + 1, 4 * b] * block)
                    add_to(
                        total8, (n, q, h), SS[e + 1, 3] * block_of(force, a * 112 + 96 + q * 8, h)
                    )
    for h in range(2):
        at = column_rows(COLS + 2 * p + h)
        for n in range(3):
            K8[n, at, :] = total8[n, 0, h] + to_next_z(total8[n, 1, h])
            for d in range(3):
                KS[d * 3 + n, at, :] = total[n, d, 0, h] + to_next_z(total[n, d, 1, h])


def put_halves(ref, row, rows_low, lanes, value):
    high, low = halves(value)
    ref[row : row + WIDE, lanes] = high
    ref[rows_low + row : rows_low + row + WIDE, lanes] = low


def gram_sums(refs):
    XS, KS, X8, K8, LM = refs["XS"], refs["KS"], refs["X8"], refs["K8"], refs["LM"]
    GX, GY, FT = refs["GX"], refs["GY"], refs["FT"]

    def product(slot, width):
        return lax.dot_general(
            GX[slot, :, 0:width],
            GY[slot, :, 0:width],
            (((1,), (1,)), ((), ())),
            preferred_element_type=F32,
        )

    total = jnp.zeros((2 * WIDE, 4 * WIDE), F32)
    for i in range(6):
        d, n = i // 2, i % 2
        for y in range(8):
            lanes = slice(y * 128, y * 128 + 128)
            rows = pl.ds(y, WIDE, stride=8)
            value = XS[d * 3 + n, rows, :]
            put_halves(GX.at[i % 2], 0, WIDE, lanes, value)
            put_halves(GY.at[i % 2], 0, 2 * WIDE, lanes, KS[d * 3 + n, rows, :])
            put_halves(GY.at[i % 2], WIDE, 2 * WIDE, lanes, value * LM[n, 0, y : y + 1])
        total = total + product(i % 2, 1024)
    for slot in range(2):
        GY[slot] = jnp.zeros(GY.shape[1:], BF16)
    for d in range(3):
        for y in range(8):
            lanes = slice(y * 128, y * 128 + 128)
            rows = pl.ds(y, WIDE, stride=8)
            put_halves(GX.at[d % 2], 0, WIDE, lanes, XS[d * 3 + 2, rows, :])
            put_halves(GY.at[d % 2], 0, 2 * WIDE, lanes, KS[d * 3 + 2, rows, :])
        total = total + product(d % 2, 1024)
    for n in range(3):
        for d in range(3):
            lanes = slice((n * 3 + d) * 128, (n * 3 + d) * 128 + 128)
            rows = pl.ds(d, WIDE, stride=8)
            put_halves(GX.at[1], 0, WIDE, lanes, X8[n, rows, :])
            put_halves(GY.at[1], 0, 2 * WIDE, lanes, K8[n, rows, :])
    total = total + product(1, 1152)
    FT[...] = jnp.zeros(FT.shape, F32)
    FT[:, 0 : 4 * WIDE] = total[0:WIDE] + total[WIDE : 2 * WIDE]
    wide = FT[...]
    stiff = wide[:, 0:128] + pltpu.roll(wide, 256 - 2 * WIDE, 1)[:, 0:128]
    mass = pltpu.roll(stiff, 128 - WIDE, 1)
    lane, row = lane_of(stiff), row_of(stiff)
    packed = jnp.where(row >= lane, stiff, mass)
    diagonal = jnp.sum(jnp.where(row == lane, mass, 0.0), axis=1, keepdims=True)
    half = WIDE // 2
    lane = lane[0:half]
    out = jnp.where(lane < WIDE, packed[0:half], pltpu.roll(packed[half:WIDE], WIDE, 1))
    out = jnp.where(lane < 2 * WIDE, out, 0.0)
    out = jnp.where(lane == 2 * WIDE, diagonal[0:half], out)
    return jnp.where(lane == 2 * WIDE + 1, diagonal[half:WIDE], out)


COMPUTE_SCRATCH = {
    "XC": ((COLS, 3, 5, 16, 128), F32),
    "XP": ((COLS, 3, 3, 16, 128), F32),
    "FE": ((2, 3, 5, 16, 128), F32),
    "modulus_in": ((2, 8, 128), F32),
    "density_in": ((2, 8, 128), F32),
    "solid_in": ((2, 8, 128), jnp.int32),
    "clamped_in": ((2, 8), jnp.int32),
    "elem_in": ((24, 24), F32),
    "rows_in": ((480, 25), F32),
    "cols_in": ((24, 1920), F32),
    "ys_in": ((8, 960), F32),
    "W1": ((256, 576), BF16),
    "W2": ((224, 384), BF16),
    "SS": ((4, 5, 8, 128), F32),
    "LM": ((3, 2, 8, 128), F32),
    "PM": ((3, 3, 8, 128), F32),
    "P8": ((3, 8, 128), F32),
    "VV": ((2, 3, 2, 3, 16, 128), F32),
    "UH": ((5, 96, 256), BF16),
    "UL": ((5, 96, 256), BF16),
    "U2H": ((3 * PAIRS, 3, 64, 256), BF16),
    "U2L": ((3 * PAIRS, 3, 64, 256), BF16),
    "XS": ((9, WIDE * 8, 128), F32),
    "KS": ((9, WIDE * 8, 128), F32),
    "X8": ((3, WIDE * 8, 128), F32),
    "K8": ((3, WIDE * 8, 128), F32),
    "GX": ((2, 2 * WIDE, 1152), BF16),
    "GY": ((2, 4 * WIDE, 1152), BF16),
    "FT": ((WIDE, 256), F32),
    "ES": ((COLS, 2, 8, 128), F32),
    "EM": ((COLS, 2, 8, 128), F32),
}


def reduce_groups(sizes):
    nx, ny = sizes
    near = min(4, nx)
    groups = [("bx", 1, near), ("bx", near, nx // near), ("by", 1, ny)]
    return [g for g in groups if g[2] > 1]


def peers_of(axis, stride, size):
    at = lax.axis_index(axis)
    place = (at // stride) % size
    base = at - place * stride
    peers = [lax.rem(place + k, size) for k in range(1, size)]
    return place, [(there, base + there * stride) for there in peers]


def greet_reducers(sizes, barrier):
    count = 0
    for axis, stride, size in reduce_groups(sizes):
        for _, peer in peers_of(axis, stride, size)[1]:
            pl.semaphore_signal(barrier, inc=1, device_id={axis: peer}, device_id_type=MESH)
            count += 1
    pl.semaphore_signal(
        barrier, inc=1, device_id={"real": 1 - lax.axis_index("real")}, device_id_type=MESH
    )
    return count + 1


def all_reduce(sizes, refs, value):
    for i, (axis, stride, size) in enumerate(reduce_groups(sizes)):
        slots = refs[f"slots{i}"]
        place, peers = peers_of(axis, stride, size)
        slots[place] = value
        copies = [
            pltpu.make_async_remote_copy(
                src_ref=slots.at[place],
                dst_ref=slots.at[place],
                send_sem=refs[f"rsend{i}"].at[k],
                recv_sem=refs[f"rrecv{i}"].at[place],
                device_id={axis: peer},
                device_id_type=MESH,
            )
            for k, (_, peer) in enumerate(peers)
        ]
        for copy in copies:
            copy.start()
        for there, peer in peers:
            pltpu.make_async_remote_copy(
                src_ref=slots.at[place],
                dst_ref=slots.at[there],
                send_sem=refs[f"rsend{i}"].at[0],
                recv_sem=refs[f"rrecv{i}"].at[there],
                device_id={axis: peer},
                device_id_type=MESH,
            ).wait_recv()
        value = slots[0]
        for k in range(1, size):
            value = value + slots[k]
        for copy in copies:
            copy.wait_send()
    return value


def quotients(value):
    diagonal = lane_of(value) == row_of(value)
    numerator = jnp.sum(jnp.where(diagonal, value, 0.0), axis=1, keepdims=True)
    denominator = value[:, 2 * WIDE : 2 * WIDE + 1]
    return numerator / denominator, denominator


def sensitivities(refs, value):
    quotient_col, denominator_col = quotients(value)
    weights, power_sum = [], jnp.zeros((1, 1), F32)
    for j in range(COLS):
        quotient = quotient_col[j : j + 1]
        inverse = 1.0 / quotient
        square = inverse * inverse
        powered = square * square
        power_sum = power_sum + powered
        weights.append((quotient, powered / denominator_col[j : j + 1]))
    terms = refs["terms"]
    for n in range(2):
        stiff_sum = jnp.zeros((8, 128), F32)
        mass_sum = jnp.zeros((8, 128), F32)
        for j, (quotient, weight) in enumerate(weights):
            stiff_sum = stiff_sum + weight * refs["ES"][j, n]
            mass_sum = mass_sum + (weight * quotient) * refs["EM"][j, n]
        terms[0, n] = (
            3.0 * refs["FE"][0, 0, n + 1, 0:8] * stiff_sum
            - refs["FE"][0, 1, n + 1, 0:8] * mass_sum
        )
    terms[0, 2] = jnp.broadcast_to(power_sum, (8, 128))
    swap = pltpu.make_async_remote_copy(
        src_ref=terms.at[0],
        dst_ref=terms.at[1],
        send_sem=refs["swap_sem"].at[0],
        recv_sem=refs["swap_sem"].at[1],
        device_id={"real": 1 - lax.axis_index("real")},
        device_id_type=MESH,
    )
    swap.start()
    swap.wait()
    overall = terms[0, 2] + terms[1, 2]
    for n in range(2):
        refs["sens_all"][n] = (terms[0, n] + terms[1, n]) / overall


def step_kernel(sizes, dofs, names, *args):
    refs = dict(zip(names, args))
    halo = Halo(sizes, refs)
    barrier = pltpu.get_barrier_semaphore()
    FE, XC, XP, local_sem = refs["FE"], refs["XC"], refs["XP"], refs["local_sem"]
    pairs = [
        (refs["modulus"], refs["modulus_in"]),
        (refs["density"], refs["density_in"]),
        (refs["solid"].at[0], refs["solid_in"]),
        (refs["clamped"], refs["clamped_in"]),
        (refs["precond"], FE.at[1:2, :, 1:3, 0:8, :]),
        (refs["cur"], XC.at[:, :, 1:3, 0:8, :]),
        (refs["prev"], XP.at[:, :, 0:2, 0:8, :]),
        *((refs[name], refs[name + "_in"]) for name in ("elem", "rows", "cols", "ys")),
    ]
    loads = [pltpu.make_async_copy(a, b, local_sem.at[k]) for k, (a, b) in enumerate(pairs)]
    for load in loads[0:4]:
        load.start()
    for k in range(2):
        FE[k] = jnp.zeros(FE.shape[1:], F32)
    loads[4].start()
    zero_rows = jnp.zeros((3, 5, 8, 128), F32)

    def clear(c, carry):
        for x in (0, 3, 4):
            XC[c, :, x, 0:8] = jnp.zeros((3, 8, 128), F32)
        XC[c, :, :, 8:16] = zero_rows
        XP[c, :, 2, 0:8] = jnp.zeros((3, 8, 128), F32)
        XP[c, :, :, 8:16] = zero_rows[:, 0:3]
        return carry

    lax.fori_loop(0, COLS, clear, 0)
    count = halo.greet(barrier) + greet_reducers(sizes, barrier)
    for load in loads[5:]:
        load.start()
    for load in loads[0:5]:
        load.wait()
    own_fields(refs)
    pl.semaphore_wait(barrier, count)
    fields, previous = halo.fields(), halo.previous()
    halo.start(fields)
    for c in range(CHUNKS):
        halo.start(halo.chunk(c))
    halo.start(previous)
    for load in loads[5:]:
        load.wait()
    build_operators(refs)
    halo.arrived(fields)
    prepare_fields(refs)

    def one(c, carry):
        halo.arrived(halo.chunk(c))

        def inner(k, carry):
            p = c * (PER_CHUNK // 2) + k
            current_pair(refs, p)
            second_pair(refs, p)
            second_pair(refs, PAIRS + p)
            return carry

        return lax.fori_loop(0, PER_CHUNK // 2, inner, carry)

    lax.fori_loop(0, CHUNKS, one, 0)
    halo.arrived(previous)

    def two(p, carry):
        previous_pair(refs, p)
        second_pair(refs, 2 * PAIRS + p)
        return carry

    lax.fori_loop(0, PAIRS, two, 0)
    value = all_reduce(sizes, refs, gram_sums(refs)) / dofs
    refs["grams"][...] = value
    sensitivities(refs, value)
    halo.left(fields)
    for c in range(CHUNKS):
        halo.left(halo.chunk(c))
    halo.left(previous)


def result_kernel(names, *args):
    refs = dict(zip(names, args))
    value = refs["grams"][...]
    quotient_col, _ = quotients(value)
    half = WIDE // 2
    packed = jnp.concatenate([value, pltpu.roll(value, 128 - WIDE, 1)], 0)
    lane, row = lane_of(packed), row_of(packed)
    masses = jnp.concatenate(
        [value[:, 2 * WIDE : 2 * WIDE + 1], value[:, 2 * WIDE + 1 : 2 * WIDE + 2]], 0
    )
    turned = jnp.transpose(jnp.concatenate([packed, jnp.zeros((128 - WIDE, 128), F32)], 0))[0:WIDE]
    stiff = jnp.where(row >= lane, packed, turned)
    mass = jnp.where(row == lane, masses, jnp.where(row > lane, turned, packed))
    wide_col = jnp.broadcast_to(quotient_col, (half, 128))
    wide_col = jnp.concatenate([wide_col, wide_col], 0)
    on_diagonal = jnp.where((lane == row) & (row < COLS), wide_col, 0.0)
    quotient_row = jnp.broadcast_to(jnp.sum(on_diagonal, axis=0, keepdims=True), (WIDE, 128))
    shifted_row = pltpu.roll(quotient_row, COLS, 1)
    shifted_col = pltpu.roll(wide_col, COLS, 0)
    for name, gram in (("gram_stiff", stiff), ("gram_mass", mass)):
        moved = pltpu.roll(gram, 128 - COLS, 1)
        side = jnp.where(
            lane < COLS, gram, jnp.where(lane < 2 * COLS, gram - shifted_row * moved, moved)
        )
        moved = pltpu.roll(side, WIDE - COLS, 0)
        full = jnp.where(
            row < COLS, side, jnp.where(row < 2 * COLS, side - shifted_col * moved, moved)
        )
        for i in range(3 * COLS):
            refs[name][i] = full[i : i + 1, 0 : 3 * COLS]
    for j in range(COLS):
        quotient = quotient_col[j : j + 1]
        for d in range(3):
            for n in range(2):
                refs["search"][0, j, d, n] = (
                    refs["first"][j, d, n] - quotient * refs["second"][j, d, n]
                )
    real = lax.axis_index("real")
    for n in range(2):
        whole = refs["sens_all"][n]
        refs["sens"][n] = jnp.where(real == 0, whole, pltpu.roll(whole, 64, 1))[:, 0:64]


VMEM_SPEC = pl.BlockSpec(memory_space=pltpu.VMEM)
HBM_SPEC = pl.BlockSpec(memory_space=pltpu.HBM)


def run(kernel, statics, ins, outs, scratch, in_hbm=False, **params):
    names = [*ins, *outs, *scratch]
    result = pl.pallas_call(
        functools.partial(kernel, *statics, names),
        out_shape=[jax.ShapeDtypeStruct(shape, dtype) for shape, dtype in outs.values()],
        in_specs=[HBM_SPEC if in_hbm else VMEM_SPEC for name in ins],
        out_specs=[VMEM_SPEC for _ in outs],
        scratch_shapes=list(scratch.values()),
        compiler_params=pltpu.CompilerParams(**params),
        name=kernel.__name__,
    )(*(pltpu.with_memory_space_constraint(v, pltpu.HBM) if in_hbm else v for v in ins.values()))
    return dict(zip(outs, result))


def step_scratch(sizes):
    out = {name: pltpu.VMEM(shape, dtype) for name, (shape, dtype) in COMPUTE_SCRATCH.items()}
    out["send_sem"] = pltpu.SemaphoreType.DMA((N_HALO,))
    out["recv_sem"] = pltpu.SemaphoreType.DMA((N_HALO,))
    out["local_sem"] = pltpu.SemaphoreType.DMA((11,))
    for i, (_, _, size) in enumerate(reduce_groups(sizes)):
        out[f"slots{i}"] = pltpu.VMEM((size, WIDE // 2, 128), F32)
        out[f"rsend{i}"] = pltpu.SemaphoreType.DMA((size,))
        out[f"rrecv{i}"] = pltpu.SemaphoreType.DMA((size,))
    out["terms"] = pltpu.VMEM((2, 3, 8, 128), F32)
    out["swap_sem"] = pltpu.SemaphoreType.DMA((2,))
    return out


def shards(sizes, current, previous, element_stiffness, preconditioner, modulus, density, solid, clamped):
    size_x, size_y, size_z = modulus.shape
    nx, ny = sizes
    dofs = 3.0 * size_x * size_y * size_z * nx * ny
    ins = dict(
        cur=current[0],
        prev=previous[0],
        precond=preconditioner,
        modulus=modulus,
        density=density,
        solid=solid,
        clamped=clamped,
        elem=element_stiffness,
        **{name: jnp.asarray(table) for name, table in operator_tables().items()},
    )
    step = run(
        step_kernel,
        (sizes, dofs),
        ins,
        dict(
            grams=((WIDE // 2, 128), F32),
            first=((COLS, 3, 2, 8, 128), F32),
            second=((COLS, 3, 2, 8, 128), F32),
            sens_all=((2, 8, 128), F32),
        ),
        step_scratch(sizes),
        in_hbm=True,
        vmem_limit_bytes=32 * 2**20,
        collective_id=1,
        has_side_effects=True,
    )
    done = run(
        result_kernel,
        (),
        step,
        dict(
            gram_stiff=((3 * COLS, 1, 3 * COLS), F32),
            gram_mass=((3 * COLS, 1, 3 * COLS), F32),
            search=((1, COLS, 3, 2, 8, 128), F32),
            sens=((2, 8, 64), F32),
        ),
        {},
        vmem_limit_bytes=8 * 2**20,
    )
    grams = [jnp.transpose(done[name], (1, 0, 2)) for name in ("gram_stiff", "gram_mass")]
    return *grams, done["search"], done["sens"]


def solution(mesh):
    sizes = (mesh.shape["bx"], mesh.shape["by"])
    return jax.shard_map(
        functools.partial(shards, sizes),
        mesh=mesh,
        in_specs=(
            P("real", None, None, "bx", "by", None),
            P("real", None, None, "bx", "by", None),
            P(),
            P("real", None, "bx", "by", None),
            P("bx", "by", None),
            P("bx", "by", None),
            P("real", "bx", "by", None),
            P("bx", "by"),
        ),
        out_specs=(
            P("real", None, None),
            P("real", None, None),
            P("real", None, None, "bx", "by", None),
            P("bx", "by", "real"),
        ),
        check_vma=False,
    )
```

time: 75.8 us -> 48.4 us (0.64)
  Pallas kernels: 64 us -> 47.7 us
  local copies, waits for them, and re-layouts: 8.4 us -> 0 us
  other arithmetic: 2.2 us -> 0 us
    pallas_call x3 -> x2, Pallas kernels: 64 us -> 47.7 us  [run(): pl.pallas_call(functools.partial(kernel, *statics, names), out_shape=[jax...]
    unnamed x6 -> x0, local copies, waits for them, and re-layouts: 5 us -> none
    pallas_call x2 -> x0, local copies, waits for them, and re-layouts: 2.7 us -> none  [run(): pl.pallas_call(functools.partial(kernel, *statics, names), out_shape=[jax...]
    unnamed x3 -> x0, other arithmetic: 1.51 us -> none
where the time goes in v2:
time: 48.4 us; the launch traced here: 48.3 us
  Pallas kernels  47.7 us (99%)
  between operations  0.64 us (1%)
    pallas_call x2, Pallas kernels, run(): pl.pallas_call(functools.partial(kernel, *statics, names), out_shape=[jax...  47.7 us

profile of v2, /device:TPU:2, one launch (start us, length us, event | category | flops | bytes accessed | tf_op | source)
XLA Modules:
  0.0 48.3 jit_solution(14116343571710508339)
XLA Ops:
  0.6 46.6 %step_kernel.1 = (f32[24,128]{1,0:T(8,128)S(1)}, f32[12,3,2,8,128]{4,3,2,1,0:T(8,128)S(1)}, f32[12,3,2,8,128]{4,3,2,1,0:T(8,128)S(1)}, f32[2,8,128]{2,1,0:T(8,128)S(1)}) custom-call(f32[12,3,2,8,128]{4,3,2,1,0:T(8,128)} %bitcast.4, f32[12,3,2,8,128]{4,3,2,1,0:T(8,128)} %bitcast.5, f32[1,3,2,8,128]{4,3,2,1,0:T(8,128)} %args_2_.4, f32[2,8,128]{2,1,0:T(8,128)} %args_3_.4, ...), custom_call_target="tpu_custom_call" | custom-call | tf_op jit(solution)/shard_map/step_kernel/pallas_call | solution.py:769
  47.3 1.0 %result_kernel.1 = (f32[36,1,36]{2,1,0:T(1,128)}, f32[36,1,36]{2,1,0:T(1,128)}, f32[1,12,3,2,8,128]{5,4,3,2,1,0:T(8,128)}, f32[2,8,64]{2,1,0:T(8,128)}) custom-call(f32[24,128]{1,0:T(8,128)S(1)} %get-tuple-element.12.args_0_, f32[12,3,2,8,128]{4,3,2,1,0:T(8,128)S(1)} %get-tuple-element.13.args_1_, f32[12,3,2,8,128]{4,3,2,1,0:T(8,128)S(1)} %get-tuple-element.14.args_2_, ...), custom_call_target="tpu_custom_call" | custom-call | tf_op jit(solution)/shard_map/result_kernel/pallas_call | solution.py:769

commit v3 on v2

--- a/solution.py
+++ b/solution.py
@@ -67,7 +67,7 @@
             second += [(a, d % 3, q, 8 if d < 3 else None) for d in range(8)]
     for rows in (first, second):
         size = 3 * len(rows)
-        pick_col = np.zeros((24, 2 * size), np.float32)
+        pick_col = np.zeros((48, 2 * size), np.float32)
         row_y = np.full((8, size), NOWHERE * 2, np.float32)
         for part in range(3):
             for k, (a, d, q, y) in enumerate(rows):
@@ -76,23 +76,21 @@
                 at = part * len(rows) + k
                 row_y[:, at] = y
                 for b in range(2):
-                    pick_col[3 * (4 * a + 2 * b + q) + d, b * size + at] = 1
+                    i = 24 * (part == 2) + 3 * (4 * a + 2 * b + q) + d
+                    pick_col[i, b * size + at] = 1
         out += [pick_col, row_y]
     row1, row2, col1, y1, col2, y2 = out
-    tables = dict(
-        rows=np.concatenate([row1, row2]), cols=np.concatenate([col1, col2], 1), ys=np.concatenate([y1, y2], 1)
+    rows = np.concatenate([row1, row2])
+    return dict(
+        rows=rows[:, 0:24],
+        row_ys=np.tile(rows[:, 24:25], (1, 128)),
+        cols=np.concatenate([col1, col2], 1),
+        col_ys=np.concatenate([y1, y2], 1),
     )
-    return tables
-
-
-def exact_dot(left, right):
-    return lax.dot_general(
-        left,
-        right,
-        (((1,), (0,)), ((), ())),
-        preferred_element_type=F32,
-        precision=lax.Precision.HIGHEST,
-    )
+
+
+def pick_dot(left, right):
+    return lax.dot_general(left, right, (((1,), (0,)), ((), ())), preferred_element_type=F32)
 
 
 def halves(value):
@@ -137,7 +135,7 @@
 
 
 def column_rows(index):
-    return pl.ds(pl.multiple_of(index * 8, 8), 8)
+    return pl.ds(index, 8, stride=WIDE)
 
 
 class Halo:
@@ -234,19 +232,22 @@
 
 
 def build_operators(refs):
+    high, low = halves(refs["elem_in"][...])
+    spread_high = pick_dot(refs["rows_in"][...], high).astype(BF16)
+    spread_low = pick_dot(refs["rows_in"][...], low).astype(BF16)
     for row, rows, at, out in ((0, 256, 0, "W1"), (256, 224, 576, "W2")):
-        table = refs["rows_in"][row : row + rows]
         size = refs[out].shape[1]
-        both = exact_dot(
-            exact_dot(table[:, 0:24], refs["elem_in"][...]),
-            refs["cols_in"][:, 2 * at : 2 * (at + size)],
-        )
-        gap = refs["ys_in"][0:1, at : at + size] - table[:, 24:25]
-        full = jnp.where(gap == 0.0, both[:, 0:size], 0.0) + jnp.where(
-            gap == 1.0, both[:, size : 2 * size], 0.0
-        )
-        high = full.astype(BF16).astype(F32)
-        refs[out][...] = jnp.where(lane_of(full) < 2 * size // 3, high, full - high).astype(BF16)
+        cols = refs["cols_in"]
+        gap = refs["col_ys_in"][0:1, at : at + size]
+        total = 0.0
+        for b in range(2):
+            columns = slice(2 * at + b * size, 2 * at + (b + 1) * size)
+            picked = pick_dot(spread_high[row : row + rows], cols[0:24, columns]) + pick_dot(
+                spread_low[row : row + rows], cols[24:48, columns]
+            )
+            match = gap - refs["row_ys_in"][row : row + rows, 0:1] == float(b)
+            total = total + jnp.where(match, picked, 0.0)
+        refs[out][...] = total.astype(BF16)
 
 
 def prepare_fields(refs):
@@ -381,6 +382,15 @@
                     refs["second"][c, d, n] = seconds[d]
             store_second(refs, (p, n), h, firsts, first8)
             store_second(refs, (PAIRS + p, n), h, seconds, second8)
+        top, bottom = 0.0, 0.0
+        for n in range(2):
+            for d in range(3):
+                here = VV[h, d, 0, n, 0:8]
+                stiff = total[n, d, 0, h] + to_next_z(total[n, d, 1, h])
+                top = top + here * stiff
+                bottom = bottom + here * here * LM[n, 0]
+        refs["QV"][pl.ds(c, 1), :] = jnp.sum(top, axis=0, keepdims=True)
+        refs["QV"][pl.ds(16 + c, 1), :] = jnp.sum(bottom, axis=0, keepdims=True)
         for e in (1, 2):
             above = jnp.sum(energy8[e, h], axis=0, keepdims=True)
             refs["ES"][c, e - 1] = energy[e, 0, h] + from_upper_y(energy[e, 1, h], above)
@@ -441,7 +451,7 @@
     ref[rows_low + row : rows_low + row + WIDE, lanes] = low
 
 
-def gram_sums(refs):
+def gram_sums(refs, between):
     XS, KS, X8, K8, LM = refs["XS"], refs["KS"], refs["X8"], refs["K8"], refs["LM"]
     GX, GY, FT = refs["GX"], refs["GY"], refs["FT"]
 
@@ -458,25 +468,27 @@
         d, n = i // 2, i % 2
         for y in range(8):
             lanes = slice(y * 128, y * 128 + 128)
-            rows = pl.ds(y, WIDE, stride=8)
+            rows = slice(y * WIDE, (y + 1) * WIDE)
             value = XS[d * 3 + n, rows, :]
             put_halves(GX.at[i % 2], 0, WIDE, lanes, value)
             put_halves(GY.at[i % 2], 0, 2 * WIDE, lanes, KS[d * 3 + n, rows, :])
             put_halves(GY.at[i % 2], WIDE, 2 * WIDE, lanes, value * LM[n, 0, y : y + 1])
         total = total + product(i % 2, 1024)
+        if i == 3:
+            between()
     for slot in range(2):
         GY[slot] = jnp.zeros(GY.shape[1:], BF16)
     for d in range(3):
         for y in range(8):
             lanes = slice(y * 128, y * 128 + 128)
-            rows = pl.ds(y, WIDE, stride=8)
+            rows = slice(y * WIDE, (y + 1) * WIDE)
             put_halves(GX.at[d % 2], 0, WIDE, lanes, XS[d * 3 + 2, rows, :])
             put_halves(GY.at[d % 2], 0, 2 * WIDE, lanes, KS[d * 3 + 2, rows, :])
         total = total + product(d % 2, 1024)
     for n in range(3):
         for d in range(3):
             lanes = slice((n * 3 + d) * 128, (n * 3 + d) * 128 + 128)
-            rows = pl.ds(d, WIDE, stride=8)
+            rows = slice(d * WIDE, (d + 1) * WIDE)
             put_halves(GX.at[1], 0, WIDE, lanes, X8[n, rows, :])
             put_halves(GY.at[1], 0, 2 * WIDE, lanes, K8[n, rows, :])
     total = total + product(1, 1152)
@@ -505,9 +517,10 @@
     "solid_in": ((2, 8, 128), jnp.int32),
     "clamped_in": ((2, 8), jnp.int32),
     "elem_in": ((24, 24), F32),
-    "rows_in": ((480, 25), F32),
-    "cols_in": ((24, 1920), F32),
-    "ys_in": ((8, 960), F32),
+    "rows_in": ((480, 24), BF16),
+    "row_ys_in": ((480, 128), F32),
+    "cols_in": ((48, 1920), BF16),
+    "col_ys_in": ((8, 960), F32),
     "W1": ((256, 576), BF16),
     "W2": ((224, 384), BF16),
     "SS": ((4, 5, 8, 128), F32),
@@ -526,6 +539,7 @@
     "GX": ((2, 2 * WIDE, 1152), BF16),
     "GY": ((2, 4 * WIDE, 1152), BF16),
     "FT": ((WIDE, 256), F32),
+    "QV": ((32, 128), F32),
     "ES": ((COLS, 2, 8, 128), F32),
     "EM": ((COLS, 2, 8, 128), F32),
 }
@@ -533,8 +547,7 @@
 
 def reduce_groups(sizes):
     nx, ny = sizes
-    near = min(4, nx)
-    groups = [("bx", 1, near), ("bx", near, nx // near), ("by", 1, ny)]
+    groups = [("bx", 1, 2), ("bx", 2, nx // 2), ("by", 1, ny)]
     return [g for g in groups if g[2] > 1]
 
 
@@ -558,50 +571,54 @@
     return count + 1
 
 
-def all_reduce(sizes, refs, value):
-    for i, (axis, stride, size) in enumerate(reduce_groups(sizes)):
-        slots = refs[f"slots{i}"]
-        place, peers = peers_of(axis, stride, size)
-        slots[place] = value
-        copies = [
-            pltpu.make_async_remote_copy(
-                src_ref=slots.at[place],
-                dst_ref=slots.at[place],
-                send_sem=refs[f"rsend{i}"].at[k],
-                recv_sem=refs[f"rrecv{i}"].at[place],
-                device_id={axis: peer},
-                device_id_type=MESH,
-            )
-            for k, (_, peer) in enumerate(peers)
-        ]
-        for copy in copies:
-            copy.start()
-        for there, peer in peers:
-            pltpu.make_async_remote_copy(
-                src_ref=slots.at[place],
-                dst_ref=slots.at[there],
-                send_sem=refs[f"rsend{i}"].at[0],
-                recv_sem=refs[f"rrecv{i}"].at[there],
-                device_id={axis: peer},
-                device_id_type=MESH,
-            ).wait_recv()
+class Reducer:
+    def __init__(self, sizes, refs, tag):
+        self.refs, self.tag, self.groups = refs, tag, reduce_groups(sizes)
+
+    def part(self, name, i):
+        return self.refs[f"{name}{self.tag}{i}"]
+
+    def copy(self, i, place, slot, peer, k):
+        return pltpu.make_async_remote_copy(
+            src_ref=self.part("slots", i).at[place],
+            dst_ref=self.part("slots", i).at[slot],
+            send_sem=self.part("rsend", i).at[k],
+            recv_sem=self.part("rrecv", i).at[slot],
+            device_id={self.groups[i][0]: peer},
+            device_id_type=MESH,
+        )
+
+    def start(self, i, value):
+        place, peers = peers_of(*self.groups[i])
+        self.part("slots", i)[place] = value
+        for k, (_, peer) in enumerate(peers):
+            self.copy(i, place, place, peer, k).start()
+
+    def end(self, i):
+        place, peers = peers_of(*self.groups[i])
+        for k, (there, peer) in enumerate(peers):
+            self.copy(i, place, there, peer, k).wait_recv()
+        slots = self.part("slots", i)
         value = slots[0]
-        for k in range(1, size):
+        for k in range(1, self.groups[i][2]):
             value = value + slots[k]
-        for copy in copies:
-            copy.wait_send()
-    return value
-
-
-def quotients(value):
-    diagonal = lane_of(value) == row_of(value)
-    numerator = jnp.sum(jnp.where(diagonal, value, 0.0), axis=1, keepdims=True)
-    denominator = value[:, 2 * WIDE : 2 * WIDE + 1]
-    return numerator / denominator, denominator
-
-
-def sensitivities(refs, value):
-    quotient_col, denominator_col = quotients(value)
+        return value
+
+    def sent(self):
+        for i, group in enumerate(self.groups):
+            place, peers = peers_of(*group)
+            for k, (_, peer) in enumerate(peers):
+                self.copy(i, place, place, peer, k).wait_send()
+
+
+def quotients(sums):
+    sums = jnp.sum(sums, axis=1, keepdims=True)
+    return sums[0:16] / sums[16:32], sums[16:32]
+
+
+def send_sensitivities(refs, dofs, sums):
+    quotient_col, denominator_col = quotients(sums)
+    denominator_col = denominator_col / dofs
     weights, power_sum = [], jnp.zeros((1, 1), F32)
     for j in range(COLS):
         quotient = quotient_col[j : j + 1]
@@ -622,16 +639,23 @@
             - refs["FE"][0, 1, n + 1, 0:8] * mass_sum
         )
     terms[0, 2] = jnp.broadcast_to(power_sum, (8, 128))
-    swap = pltpu.make_async_remote_copy(
-        src_ref=terms.at[0],
-        dst_ref=terms.at[1],
+    swap_of(refs).start()
+
+
+def swap_of(refs):
+    return pltpu.make_async_remote_copy(
+        src_ref=refs["terms"].at[0],
+        dst_ref=refs["terms"].at[1],
         send_sem=refs["swap_sem"].at[0],
         recv_sem=refs["swap_sem"].at[1],
         device_id={"real": 1 - lax.axis_index("real")},
         device_id_type=MESH,
     )
-    swap.start()
-    swap.wait()
+
+
+def end_sensitivities(refs):
+    swap_of(refs).wait()
+    terms = refs["terms"]
     overall = terms[0, 2] + terms[1, 2]
     for n in range(2):
         refs["sens_all"][n] = (terms[0, n] + terms[1, n]) / overall
@@ -650,11 +674,13 @@
         (refs["precond"], FE.at[1:2, :, 1:3, 0:8, :]),
         (refs["cur"], XC.at[:, :, 1:3, 0:8, :]),
         (refs["prev"], XP.at[:, :, 0:2, 0:8, :]),
-        *((refs[name], refs[name + "_in"]) for name in ("elem", "rows", "cols", "ys")),
+        *((refs[name], refs[name + "_in"]) for name in ("elem", "rows", "row_ys", "cols", "col_ys")),
     ]
     loads = [pltpu.make_async_copy(a, b, local_sem.at[k]) for k, (a, b) in enumerate(pairs)]
     for load in loads[0:4]:
         load.start()
+    count = greet_reducers(sizes, barrier)
+    refs["QV"][...] = jnp.zeros((32, 128), F32)
     for k in range(2):
         FE[k] = jnp.zeros(FE.shape[1:], F32)
     loads[4].start()
@@ -669,7 +695,7 @@
         return carry
 
     lax.fori_loop(0, COLS, clear, 0)
-    count = halo.greet(barrier) + greet_reducers(sizes, barrier)
+    count = count + halo.greet(barrier)
     for load in loads[5:]:
         load.start()
     for load in loads[0:5]:
@@ -678,50 +704,79 @@
     pl.semaphore_wait(barrier, count)
     fields, previous = halo.fields(), halo.previous()
     halo.start(fields)
-    for c in range(CHUNKS):
+    halo.start(halo.chunk(0))
+    halo.start(previous)
+
+    def send(c, carry):
         halo.start(halo.chunk(c))
-    halo.start(previous)
+        return carry
+
+    lax.fori_loop(1, CHUNKS, send, 0)
     for load in loads[5:]:
         load.wait()
     build_operators(refs)
     halo.arrived(fields)
     prepare_fields(refs)
 
-    def one(c, carry):
-        halo.arrived(halo.chunk(c))
-
-        def inner(k, carry):
-            p = c * (PER_CHUNK // 2) + k
-            current_pair(refs, p)
-            second_pair(refs, p)
-            second_pair(refs, PAIRS + p)
-            return carry
-
-        return lax.fori_loop(0, PER_CHUNK // 2, inner, carry)
-
-    lax.fori_loop(0, CHUNKS, one, 0)
-    halo.arrived(previous)
-
-    def two(p, carry):
+    def earlier(p, carry):
         previous_pair(refs, p)
         second_pair(refs, 2 * PAIRS + p)
         return carry
 
-    lax.fori_loop(0, PAIRS, two, 0)
-    value = all_reduce(sizes, refs, gram_sums(refs)) / dofs
-    refs["grams"][...] = value
-    sensitivities(refs, value)
+    halo.arrived(halo.chunk(0))
+    current_pair(refs, 0)
+
+    def one(p, carry):
+        @pl.when(p == PER_CHUNK // 2)
+        def _():
+            halo.arrived(previous)
+            lax.fori_loop(0, PAIRS, earlier, 0)
+
+        @pl.when(p % (PER_CHUNK // 2) == 0)
+        def _():
+            halo.arrived(halo.chunk(p // (PER_CHUNK // 2)))
+
+        second_pair(refs, p - 1)
+        second_pair(refs, PAIRS + p - 1)
+        current_pair(refs, p)
+        return carry
+
+    lax.fori_loop(1, PAIRS, one, 0)
+    second_pair(refs, PAIRS - 1)
+    second_pair(refs, 2 * PAIRS - 1)
+    early, late = Reducer(sizes, refs, "q"), Reducer(sizes, refs, "g")
+    stages = len(early.groups)
+    early.start(0, refs["QV"][...])
+
+    def between():
+        early.start(1, early.end(0))
+
+    late.start(0, gram_sums(refs, between))
+    for i in range(1, stages):
+        late.start(i, late.end(i - 1))
+        sums = early.end(i)
+        if i + 1 < stages:
+            early.start(i + 1, sums)
+    refs["sums"][...] = sums
+    send_sensitivities(refs, dofs, sums)
+    refs["grams"][...] = late.end(stages - 1) / dofs
+    end_sensitivities(refs)
+    early.sent()
+    late.sent()
     halo.left(fields)
-    for c in range(CHUNKS):
+    halo.left(previous)
+
+    def sent(c, carry):
         halo.left(halo.chunk(c))
-    halo.left(previous)
+        return carry
+
+    lax.fori_loop(0, CHUNKS, sent, 0)
 
 
 def result_kernel(names, *args):
     refs = dict(zip(names, args))
     value = refs["grams"][...]
-    quotient_col, _ = quotients(value)
-    half = WIDE // 2
+    quotient_col, _ = quotients(refs["sums"][...])
     packed = jnp.concatenate([value, pltpu.roll(value, 128 - WIDE, 1)], 0)
     lane, row = lane_of(packed), row_of(packed)
     masses = jnp.concatenate(
@@ -730,8 +785,8 @@
     turned = jnp.transpose(jnp.concatenate([packed, jnp.zeros((128 - WIDE, 128), F32)], 0))[0:WIDE]
     stiff = jnp.where(row >= lane, packed, turned)
     mass = jnp.where(row == lane, masses, jnp.where(row > lane, turned, packed))
-    wide_col = jnp.broadcast_to(quotient_col, (half, 128))
-    wide_col = jnp.concatenate([wide_col, wide_col], 0)
+    wide_col = jnp.broadcast_to(quotient_col, (16, 128))
+    wide_col = jnp.concatenate([wide_col, wide_col, wide_col], 0)
     on_diagonal = jnp.where((lane == row) & (row < COLS), wide_col, 0.0)
     quotient_row = jnp.broadcast_to(jnp.sum(on_diagonal, axis=0, keepdims=True), (WIDE, 128))
     shifted_row = pltpu.roll(quotient_row, COLS, 1)
@@ -782,11 +837,12 @@
     out = {name: pltpu.VMEM(shape, dtype) for name, (shape, dtype) in COMPUTE_SCRATCH.items()}
     out["send_sem"] = pltpu.SemaphoreType.DMA((N_HALO,))
     out["recv_sem"] = pltpu.SemaphoreType.DMA((N_HALO,))
-    out["local_sem"] = pltpu.SemaphoreType.DMA((11,))
+    out["local_sem"] = pltpu.SemaphoreType.DMA((12,))
     for i, (_, _, size) in enumerate(reduce_groups(sizes)):
-        out[f"slots{i}"] = pltpu.VMEM((size, WIDE // 2, 128), F32)
-        out[f"rsend{i}"] = pltpu.SemaphoreType.DMA((size,))
-        out[f"rrecv{i}"] = pltpu.SemaphoreType.DMA((size,))
+        for tag, rows in (("q", 32), ("g", WIDE // 2)):
+            out[f"slots{tag}{i}"] = pltpu.VMEM((size, rows, 128), F32)
+            out[f"rsend{tag}{i}"] = pltpu.SemaphoreType.DMA((size,))
+            out[f"rrecv{tag}{i}"] = pltpu.SemaphoreType.DMA((size,))
     out["terms"] = pltpu.VMEM((2, 3, 8, 128), F32)
     out["swap_sem"] = pltpu.SemaphoreType.DMA((2,))
     return out
@@ -805,7 +861,10 @@
         solid=solid,
         clamped=clamped,
         elem=element_stiffness,
-        **{name: jnp.asarray(table) for name, table in operator_tables().items()},
+        **{
+            name: jnp.asarray(table, COMPUTE_SCRATCH[name + "_in"][1])
+            for name, table in operator_tables().items()
+        },
     )
     step = run(
         step_kernel,
@@ -813,6 +872,7 @@
         ins,
         dict(
             grams=((WIDE // 2, 128), F32),
+            sums=((32, 128), F32),
             first=((COLS, 3, 2, 8, 128), F32),
             second=((COLS, 3, 2, 8, 128), F32),
             sens_all=((2, 8, 128), F32),

time: 48.4 us -> 45.2 us (0.934)
  Pallas kernels: 47.7 us -> 44.4 us
    pallas_call x2, Pallas kernels: 47.7 us -> 44.4 us  [run(): pl.pallas_call(functools.partial(kernel, *statics, names), out_shape=[jax...]
where the time goes in v3:
time: 45.2 us; the launch traced here: 45 us
  Pallas kernels  44.4 us (98%)
  between operations  0.64 us (1%)
    pallas_call x2, Pallas kernels, run(): pl.pallas_call(functools.partial(kernel, *statics, names), out_shape=[jax...  44.4 us

profile of v3, /device:TPU:2, one launch (start us, length us, event | category | flops | bytes accessed | tf_op | source)
XLA Modules:
  0.0 45.0 jit_solution(4846317756265139291)
XLA Ops:
  0.6 43.4 %step_kernel.1 = (f32[24,128]{1,0:T(8,128)S(1)}, f32[32,128]{1,0:T(8,128)S(1)}, f32[12,3,2,8,128]{4,3,2,1,0:T(8,128)S(1)}, f32[12,3,2,8,128]{4,3,2,1,0:T(8,128)S(1)}, f32[2,8,128]{2,1,0:T(8,128)S(1)}) custom-call(f32[12,3,2,8,128]{4,3,2,1,0:T(8,128)} %bitcast.4, f32[12,3,2,8,128]{4,3,2,1,0:T(8,128)} %bitcast.5, f32[1,3,2,8,128]{4,3,2,1,0:T(8,128)} %args_2_.4, ...), custom_call_target="tpu_custom_call" | custom-call | tf_op jit(solution)/shard_map/step_kernel/pallas_call | solution.py:824
  44.0 1.0 %result_kernel.1 = (f32[36,1,36]{2,1,0:T(1,128)}, f32[36,1,36]{2,1,0:T(1,128)}, f32[1,12,3,2,8,128]{5,4,3,2,1,0:T(8,128)}, f32[2,8,64]{2,1,0:T(8,128)}) custom-call(f32[24,128]{1,0:T(8,128)S(1)} %get-tuple-element.13.args_0_, f32[32,128]{1,0:T(8,128)S(1)} %get-tuple-element.14.args_1_, f32[12,3,2,8,128]{4,3,2,1,0:T(8,128)S(1)} %get-tuple-element.15.args_2_, ...), custom_call_target="tpu_custom_call" | custom-call | tf_op jit(solution)/shard_map/result_kernel/pallas_call | solution.py:824

commit v4 on v3

--- a/solution.py
+++ b/solution.py
@@ -604,9 +604,9 @@
             value = value + slots[k]
         return value
 
-    def sent(self):
-        for i, group in enumerate(self.groups):
-            place, peers = peers_of(*group)
+    def sent(self, stages):
+        for i in stages:
+            place, peers = peers_of(*self.groups[i])
             for k, (_, peer) in enumerate(peers):
                 self.copy(i, place, place, peer, k).wait_send()
 
@@ -718,13 +718,12 @@
     halo.arrived(fields)
     prepare_fields(refs)
 
+    halo.arrived(halo.chunk(0))
+    current_pair(refs, 0)
+
     def earlier(p, carry):
         previous_pair(refs, p)
-        second_pair(refs, 2 * PAIRS + p)
         return carry
-
-    halo.arrived(halo.chunk(0))
-    current_pair(refs, 0)
 
     def one(p, carry):
         @pl.when(p == PER_CHUNK // 2)
@@ -738,39 +737,41 @@
 
         second_pair(refs, p - 1)
         second_pair(refs, PAIRS + p - 1)
+        second_pair(refs, 2 * PAIRS + jnp.maximum(p - 2, 0))
         current_pair(refs, p)
         return carry
 
     lax.fori_loop(1, PAIRS, one, 0)
-    second_pair(refs, PAIRS - 1)
-    second_pair(refs, 2 * PAIRS - 1)
+    for pair in (PAIRS - 1, 2 * PAIRS - 1, 3 * PAIRS - 2, 3 * PAIRS - 1):
+        second_pair(refs, pair)
     early, late = Reducer(sizes, refs, "q"), Reducer(sizes, refs, "g")
     stages = len(early.groups)
     early.start(0, refs["QV"][...])
 
+    def sent(c, carry):
+        halo.left(halo.chunk(c))
+        return carry
+
     def between():
         early.start(1, early.end(0))
 
     late.start(0, gram_sums(refs, between))
+    halo.left(fields)
+    halo.left(previous)
     for i in range(1, stages):
         late.start(i, late.end(i - 1))
+        if i == 1:
+            lax.fori_loop(0, CHUNKS, sent, 0)
         sums = early.end(i)
         if i + 1 < stages:
             early.start(i + 1, sums)
     refs["sums"][...] = sums
     send_sensitivities(refs, dofs, sums)
+    early.sent(range(stages))
+    late.sent(range(stages - 1))
     refs["grams"][...] = late.end(stages - 1) / dofs
     end_sensitivities(refs)
-    early.sent()
-    late.sent()
-    halo.left(fields)
-    halo.left(previous)
-
-    def sent(c, carry):
-        halo.left(halo.chunk(c))
-        return carry
-
-    lax.fori_loop(0, CHUNKS, sent, 0)
+    late.sent(range(stages - 1, stages))
 
 
 def result_kernel(names, *args):

time: 45.2 us -> 44.5 us (0.985)
  Pallas kernels: 44.4 us -> 43.8 us
    pallas_call x2, Pallas kernels: 44.4 us -> 43.8 us  [run(): pl.pallas_call(functools.partial(kernel, *statics, names), out_shape=[jax...]
where the time goes in v4:
time: 44.5 us; the launch traced here: 44.4 us
  Pallas kernels  43.8 us (98%)
  between operations  0.64 us (1%)
    pallas_call x2, Pallas kernels, run(): pl.pallas_call(functools.partial(kernel, *statics, names), out_shape=[jax...  43.8 us

profile of v4, /device:TPU:2, one launch (start us, length us, event | category | flops | bytes accessed | tf_op | source)
XLA Modules:
  0.0 44.4 jit_solution(16263201470659367796)
XLA Ops:
  0.6 42.8 %step_kernel.1 = (f32[24,128]{1,0:T(8,128)S(1)}, f32[32,128]{1,0:T(8,128)S(1)}, f32[12,3,2,8,128]{4,3,2,1,0:T(8,128)S(1)}, f32[12,3,2,8,128]{4,3,2,1,0:T(8,128)S(1)}, f32[2,8,128]{2,1,0:T(8,128)S(1)}) custom-call(f32[12,3,2,8,128]{4,3,2,1,0:T(8,128)} %bitcast.4, f32[12,3,2,8,128]{4,3,2,1,0:T(8,128)} %bitcast.5, f32[1,3,2,8,128]{4,3,2,1,0:T(8,128)} %args_2_.4, ...), custom_call_target="tpu_custom_call" | custom-call | tf_op jit(solution)/shard_map/step_kernel/pallas_call | solution.py:825
  43.4 1.0 %result_kernel.1 = (f32[36,1,36]{2,1,0:T(1,128)}, f32[36,1,36]{2,1,0:T(1,128)}, f32[1,12,3,2,8,128]{5,4,3,2,1,0:T(8,128)}, f32[2,8,64]{2,1,0:T(8,128)}) custom-call(f32[24,128]{1,0:T(8,128)S(1)} %get-tuple-element.13.args_0_, f32[32,128]{1,0:T(8,128)S(1)} %get-tuple-element.14.args_1_, f32[12,3,2,8,128]{4,3,2,1,0:T(8,128)S(1)} %get-tuple-element.15.args_2_, ...), custom_call_target="tpu_custom_call" | custom-call | tf_op jit(solution)/shard_map/result_kernel/pallas_call | solution.py:825

commit v5 on v4

--- a/solution.py
+++ b/solution.py
@@ -296,7 +296,7 @@
     low_ref[at] = low
 
 
-def store_second(refs, lead, h, planes, edge):
+def store_second(refs, kind, lead, h, planes, edge):
     moved = [from_next_z(plane) for plane in planes]
     blocks = [
         (planes[0], planes[1]),
@@ -305,7 +305,9 @@
         (edge, from_next_z(edge)),
     ]
     for k, block in enumerate(blocks):
-        store_halves(refs["U2H"], refs["U2L"], lead, k * 16, h, jnp.concatenate(block, 0))
+        store_halves(
+            refs[f"U2H{kind}"], refs[f"U2L{kind}"], lead, k * 16, h, jnp.concatenate(block, 0)
+        )
 
 
 def current_pair(refs, p):
@@ -380,8 +382,8 @@
                 if n < 2:
                     refs["first"][c, d, n] = firsts[d]
                     refs["second"][c, d, n] = seconds[d]
-            store_second(refs, (p, n), h, firsts, first8)
-            store_second(refs, (PAIRS + p, n), h, seconds, second8)
+            store_second(refs, 0, (p, n), h, firsts, first8)
+            store_second(refs, 1, (p, n), h, seconds, second8)
         top, bottom = 0.0, 0.0
         for n in range(2):
             for d in range(3):
@@ -416,15 +418,15 @@
                 rows.append(value[8:9])
             edge = stacked_rows(rows)
             refs["X8"][n, at, :] = edge
-            store_second(refs, (2 * PAIRS + p, n), h, planes, edge)
-
-
-def second_pair(refs, p):
+            store_second(refs, 2, (p, n), h, planes, edge)
+
+
+def second_pair(refs, kind, p):
     SS, KS, K8 = refs["SS"], refs["KS"], refs["K8"]
     total, total8 = {}, {}
     for e in range(2):
-        high = refs["U2H"][p, e : e + 2].reshape(128, 256)
-        low = refs["U2L"][p, e : e + 2].reshape(128, 256)
+        high = refs[f"U2H{kind}"][p, e : e + 2].reshape(128, 256)
+        low = refs[f"U2L{kind}"][p, e : e + 2].reshape(128, 256)
         force = forces(refs["W2"][...], high, low)
         for a in range(2):
             n = e + a
@@ -438,7 +440,7 @@
                         total8, (n, q, h), SS[e + 1, 3] * block_of(force, a * 112 + 96 + q * 8, h)
                     )
     for h in range(2):
-        at = column_rows(COLS + 2 * p + h)
+        at = column_rows((kind + 1) * COLS + 2 * p + h)
         for n in range(3):
             K8[n, at, :] = total8[n, 0, h] + to_next_z(total8[n, 1, h])
             for d in range(3):
@@ -530,8 +532,7 @@
     "VV": ((2, 3, 2, 3, 16, 128), F32),
     "UH": ((5, 96, 256), BF16),
     "UL": ((5, 96, 256), BF16),
-    "U2H": ((3 * PAIRS, 3, 64, 256), BF16),
-    "U2L": ((3 * PAIRS, 3, 64, 256), BF16),
+    **{f"U2{part}{kind}": ((PAIRS, 3, 64, 256), BF16) for part in "HL" for kind in range(3)},
     "XS": ((9, WIDE * 8, 128), F32),
     "KS": ((9, WIDE * 8, 128), F32),
     "X8": ((3, WIDE * 8, 128), F32),
@@ -735,15 +736,15 @@
         def _():
             halo.arrived(halo.chunk(p // (PER_CHUNK // 2)))
 
-        second_pair(refs, p - 1)
-        second_pair(refs, PAIRS + p - 1)
-        second_pair(refs, 2 * PAIRS + jnp.maximum(p - 2, 0))
+        second_pair(refs, 0, p - 1)
+        second_pair(refs, 1, p - 1)
         current_pair(refs, p)
+        second_pair(refs, 2, jnp.maximum(p - 2, 0))
         return carry
 
     lax.fori_loop(1, PAIRS, one, 0)
-    for pair in (PAIRS - 1, 2 * PAIRS - 1, 3 * PAIRS - 2, 3 * PAIRS - 1):
-        second_pair(refs, pair)
+    for kind, pair in ((0, PAIRS - 1), (1, PAIRS - 1), (2, PAIRS - 2), (2, PAIRS - 1)):
+        second_pair(refs, kind, pair)
     early, late = Reducer(sizes, refs, "q"), Reducer(sizes, refs, "g")
     stages = len(early.groups)
     early.start(0, refs["QV"][...])

time: 44.5 us -> 44.3 us (level)
  no operation moved by 1% of the time
where the time goes in v5:
time: 44.3 us; the launch traced here: 44.1 us
  Pallas kernels  43.5 us (98%)
  between operations  0.64 us (1%)
    pallas_call x2, Pallas kernels, run(): pl.pallas_call(functools.partial(kernel, *statics, names), out_shape=[jax...  43.5 us

profile of v5, /device:TPU:2, one launch (start us, length us, event | category | flops | bytes accessed | tf_op | source)
XLA Modules:
  0.0 44.1 jit_solution(14195004537715896928)
XLA Ops:
  0.6 42.5 %step_kernel.1 = (f32[24,128]{1,0:T(8,128)S(1)}, f32[32,128]{1,0:T(8,128)S(1)}, f32[12,3,2,8,128]{4,3,2,1,0:T(8,128)S(1)}, f32[12,3,2,8,128]{4,3,2,1,0:T(8,128)S(1)}, f32[2,8,128]{2,1,0:T(8,128)S(1)}) custom-call(f32[12,3,2,8,128]{4,3,2,1,0:T(8,128)} %bitcast.4, f32[12,3,2,8,128]{4,3,2,1,0:T(8,128)} %bitcast.5, f32[1,3,2,8,128]{4,3,2,1,0:T(8,128)} %args_2_.4, ...), custom_call_target="tpu_custom_call" | custom-call | tf_op jit(solution)/shard_map/step_kernel/pallas_call | solution.py:826
  43.1 1.0 %result_kernel.1 = (f32[36,1,36]{2,1,0:T(1,128)}, f32[36,1,36]{2,1,0:T(1,128)}, f32[1,12,3,2,8,128]{5,4,3,2,1,0:T(8,128)}, f32[2,8,64]{2,1,0:T(8,128)}) custom-call(f32[24,128]{1,0:T(8,128)S(1)} %get-tuple-element.13.args_0_, f32[32,128]{1,0:T(8,128)S(1)} %get-tuple-element.14.args_1_, f32[12,3,2,8,128]{4,3,2,1,0:T(8,128)S(1)} %get-tuple-element.15.args_2_, ...), custom_call_target="tpu_custom_call" | custom-call | tf_op jit(solution)/shard_map/result_kernel/pallas_call | solution.py:826
